TPU v7x, 128 devices: a whole 4x4x4 slice. The times are simulated.
128 devices in a mesh: row: 16 (over y, z_lo, core), col: 8 (over z_hi, x).
Axes of the slice: x: 4, y: 4, z: 4 (z_hi: 2, z_lo: 2; z = z_hi * 2 + z_lo), core: 2. Of those that a mesh axis runs over, the one named last changes fastest.
Arguments:
- samples: bfloat16 [32768, 8192], P(('row', 'col'))
- labels: int32 [32768], P(('row', 'col')), may hold values from 0 to 1
- basis_start: bfloat16 [8192, 256], replicated, may hold values from -0.0625 to 0.0625
- width_index: int32 [], replicated, may hold values from 0 to 2
Outputs:
- projected: bfloat16 [32768, 256], P(('row', 'col'))
- proof: float32 [32768], P(('row', 'col'))
- basis: bfloat16 [8192, 256], replicated
All inputs are finite; a program needn't handle non-finite values.
Results may differ from a plain program's by a relative error of at most 0.011.
Values may be sent and summed in bfloat16 or wider, within the bound.
A program may use at most 128 MiB of HBM per device.

v0:
```python
import math

import jax
import jax.numpy as jnp
from jax import lax
from jax.sharding import PartitionSpec as P


def kernel_sums(panel_rows, panel_cols, col_is_ref, width_sq):
    row_norms = jnp.sum(jnp.square(panel_rows.astype(jnp.float32)), 1)
    col_norms = jnp.sum(jnp.square(panel_cols.astype(jnp.float32)), 1)
    block_size = math.gcd(panel_rows.shape[0], 512)

    def block_sums(pieces):
        block_rows, block_norms = pieces
        inner_products = lax.dot_general(
            block_rows, panel_cols, (((1,), (1,)), ((), ())), preferred_element_type=jnp.float32
        )
        dist_sq = block_norms[:, None] + col_norms[None, :] - 2.0 * inner_products
        kernel = jnp.exp(-dist_sq / (2.0 * width_sq))
        return (jnp.sum(kernel * col_is_ref[None, :], 1), jnp.sum(kernel, 1))

    ref_sums, row_sums = lax.map(
        block_sums,
        (
            panel_rows.reshape(-1, block_size, panel_rows.shape[1]),
            row_norms.reshape(-1, block_size),
        ),
    )
    return (ref_sums.reshape(-1), row_sums.reshape(-1))


def local(samples, labels, basis_start, width_index):
    n_total = jnp.float32(samples.shape[0] * lax.axis_size(("row", "col")))
    is_ref = (labels == 0).astype(jnp.float32)
    column_total, n_ref = lax.psum(
        (jnp.sum(samples, 0, dtype=jnp.float32), jnp.sum(is_ref)), ("row", "col")
    )
    n_cur = n_total - n_ref
    sample_mean = column_total / n_total
    centred = (samples - sample_mean).astype(jnp.bfloat16)
    first = jnp.dot(centred, basis_start, preferred_element_type=jnp.float32).astype(jnp.bfloat16)
    gram_part = (
        lax.dot_general(
            centred, first, (((0,), (0,)), ((), ())), preferred_element_type=jnp.float32
        )
        / n_total
    )
    gram = lax.psum(gram_part, ("row", "col"))
    square = jnp.dot(gram.T, gram, precision=lax.Precision.HIGHEST)
    factor = jnp.linalg.cholesky(square)
    basis = jax.scipy.linalg.solve_triangular(factor, gram.T, lower=True).T.astype(jnp.bfloat16)
    projected = jnp.dot(centred, basis, preferred_element_type=jnp.float32).astype(jnp.bfloat16)
    width_sq = 128.0 * jnp.exp2(width_index.astype(jnp.float32))
    panel_rows = lax.all_gather(projected, "col", axis=0, tiled=True)
    panel_cols, col_is_ref = (
        lax.all_gather(projected, "row", axis=0, tiled=True),
        lax.all_gather(is_ref.astype(jnp.bfloat16), "row", axis=0, tiled=True).astype(is_ref.dtype),
    )
    part_ref, part_rows = kernel_sums(panel_rows, panel_cols, col_is_ref, width_sq)
    ref_sums, row_sums = (
        lax.psum_scatter(part_ref, "col", scatter_dimension=0, tiled=True),
        lax.psum_scatter(part_rows, "col", scatter_dimension=0, tiled=True),
    )
    proof = (ref_sums / n_ref - (row_sums - ref_sums) / n_cur) / (row_sums / n_total)
    return (projected, proof, basis)


def solution(mesh):
    placed = (P(("row", "col"), None), P(("row", "col")), P(), P())
    return jax.shard_map(
        local,
        mesh=mesh,
        in_specs=placed,
        out_specs=(P(("row", "col"), None), P(("row", "col")), P()),
        check_vma=False,
    )
```

profile of v0, /device:TPU:0, one launch (start us, length us, event | category | flops | bytes accessed | tf_op | source)
XLA Modules:
  0.0 501.3 jit_solution(13970861167934475783)
XLA Ops:
  7.2 0.0 all-reduce.7.cloned.1.call-start
  7.2 2.9 convert_reduce_fusion
  10.1 0.6 fusion.26
  10.7 68.6 %all-reduce.3 = (f32[8192]{0:T(1024)S(1)}, f32[]{:T(128)}) all-reduce(f32[8192]{0:T(1024)S(1)} %convert_reduce_fusion, f32[]{:T(128)} %fusion.26), channel_id=1, replica_groups=mesh['row'=16,'col'=8] {'row','col'}, use_global_device_ids=true, to_apply=%region_1.0 | all-reduce | flops 8193 | bytes 65544 | tf_op jit(solution)/shard_map/psum | solution.py:36
  79.3 12.5 %convolution_multiply_fusion = f32[8192,256]{1,0:T(8,128)} fusion(bf16[256,8192]{1,0:T(8,128)(2,1)} %param.6, f32[8192]{0:T(1024)S(1)} %broadcast_multiply_fusion, bf16[8192,256]{1,0:T(8,128)(2,1)} %param.8), kind=kOutput, calls=%fused_computation.8 | convolution fusion | flops 2162229248 | bytes 16809984 | tf_op jit(solution)/shard_map/dot_general | solution.py:44
  91.8 0.6 all-gather.4.cloned.1.call-start
  92.4 157.5 %all-reduce.7.cloned.1.call-done = f32[8192,256]{1,0:T(8,128)} async-done(((f32[8192,256]{1,0:T(8,128)}), f32[8192,256]{1,0:T(8,128)}) %all-reduce.7.cloned.1.call-update) | async-done | bytes 8388624 | tf_op jit(solution)/shard_map/psum | solution.py:49
  249.9 19.2 %fusion.32 = f32[256,256]{1,0:T(8,128)S(1)} fusion(f32[8192,256]{1,0:T(8,128)} %all-reduce.7.cloned.1.call-done), kind=kOutput, calls=%fused_computation.55 | convolution fusion | flops 6442450944 | bytes 8650752 | tf_op jit(solution)/shard_map/dot_general | solution.py:50
  269.1 0.1 copy.9
  269.3 11.7 %cholesky.50 = f32[128,128]{1,0:T(8,128)S(1)} custom-call(f32[128,128]{1,0:T(8,128)S(1)} %cholesky.118), custom_call_target="Cholesky" | custom-call | tf_op jit(solution)/shard_map/jit(cholesky)/cholesky | solution.py:51
  281.1 9.8 %custom-call.15 = f32[1,128,128]{1,2,0:T(8,128)S(1)} custom-call(f32[1,128,128]{2,1,0:T(8,128)S(1)} %get-tuple-element.162), custom_call_target="InvertDiagBlocksLowerTriangular" | custom-call | tf_op jit(solution)/shard_map/jit(cholesky)/cholesky | solution.py:51
  290.9 0.2 constant_dynamic-update-slice_fusion.1
  291.1 0.3 convolution_subtract_fusion.1
  291.4 11.7 %cholesky.105 = f32[128,128]{1,0:T(8,128)S(1)} custom-call(f32[128,128]{1,0:T(8,128)S(1)} %convolution_subtract_fusion.1), custom_call_target="Cholesky" | custom-call | tf_op jit(solution)/shard_map/jit(cholesky)/cholesky | solution.py:51
  303.1 0.6 compare_reduce_fusion
  305.1 0.1 triangular_solve.59
  305.2 4.0 while.16
  305.2 0.6 fusion.46
  305.8 1.4 bitcast_dynamic-update-slice_fusion.2
  307.2 0.6 fusion.46
  307.8 1.4 bitcast_dynamic-update-slice_fusion.2
  309.2 19.9 %custom-call.16 = f32[2,128,128]{1,2,0:T(8,128)S(1)} custom-call(f32[2,128,128]{2,1,0:T(8,128)S(1)} %get-tuple-element.118), custom_call_target="InvertDiagBlocksLowerTriangular" | custom-call | tf_op jit(solution)/shard_map/jit(_solve_triangular)/triangular_solve | solution.py:52
  329.1 5.7 %fusion.31 = (bf16[128,8192]{1,0:T(8,128)(2,1)S(1)}, f32[128,8192]{1,0:T(8,128)S(1)}) fusion(f32[256,8192]{0,1:T(8,128)} %bitcast.65, f32[2,128,128]{1,2,0:T(8,128)S(1)} %custom-call.16), kind=kOutput, calls=%fused_computation.54 | convolution fusion | flops 1611661312 | bytes 10551296 | tf_op jit(solution)/shard_map/jit(_solve_triangular)/triangular_solve | solution.py:52
  334.8 6.7 %convolution_subtract_fusion = f32[128,8192]{0,1:T(8,128)S(1)} fusion(f32[128,8192]{1,0:T(8,128)S(1)} %get-tuple-element.166, f32[256,8192]{0,1:T(8,128)S(1)} %bitcast.66, f32[256,256]{1,0:T(8,128)S(1)} %get-tuple-element.312), kind=kOutput, calls=%fused_computation.11 | convolution fusion | flops 1611661312 | bytes 12648448 | tf_op jit(solution)/shard_map/jit(_solve_triangular)/triangular_solve | solution.py:52
  341.5 4.2 convolution_convert_fusion
  345.7 1.3 copy-done.2
  347.0 2.1 fusion.15
  349.1 0.0 all-gather.6.cloned.1.call-start
  349.2 0.7 all-gather.6.cloned.1.call-update
  349.9 17.6 %all-gather = bf16[16,1,256]{2,1,0:T(2,128)(2,1)S(1)} all-gather(bf16[1,1,256]{2,1,0:T(2,128)(2,1)S(1)} %reshape.65), channel_id=1, replica_groups=mesh['row'=16,'col'=8] {'row'}, dimensions={0}, use_global_device_ids=true | all-gather | bytes 8704 | tf_op jit(solution)/shard_map/all_gather | solution.py:58
  368.8 0.7 dynamic-slice.3
  370.1 3.9 fusion.11
  374.0 6.4 %copy.10 = bf16[8192,256]{1,0:T(8,128)(2,1)} copy(bf16[8192,256]{0,1:T(8,128)(2,1)} %fusion.11) | data formatting | bytes 8388608
  380.4 14.3 %all-gather.4.cloned.1.call-done = bf16[2048,256]{1,0:T(8,128)(2,1)} async-done(((bf16[256,256]{1,0:T(8,128)(2,1)}), bf16[2048,256]{1,0:T(8,128)(2,1)}) %all-gather.4.cloned.1.call-update) | async-done | bytes 1048592 | tf_op jit(solution)/shard_map/all_gather | solution.py:55
  394.6 1.6 multiply_reduce_fusion.2
  396.2 33.2 %all-gather.6.cloned.1.call-done = bf16[4096,256]{1,0:T(8,128)(2,1)} async-done(((bf16[256,256]{1,0:T(8,128)(2,1)}), bf16[4096,256]{1,0:T(8,128)(2,1)}) %all-gather.6.cloned.1.call-update) | async-done | bytes 2097168 | tf_op jit(solution)/shard_map/all_gather | solution.py:57
  429.4 2.2 multiply_reduce_fusion.1
  431.6 19.9 %while.15 = (s32[]{:T(128)}, f32[4,512]{1,0:T(4,128)S(1)}, f32[4,512]{1,0:T(4,128)S(1)}, f32[4,512]{1,0:T(4,128)S(1)}, f32[4096]{0:T(1024)S(1)}, /*index=5*/bf16...) while((s32[]{:T(128)}, f32[4,512]{1,0:T(4,128)S(1)}, ...), condition=%wide.region_12.13_spmd, body=%wide.region_9.12_spmd.sunk | while | flops 1090518016 | bytes 2411641 | solution.py:23
  431.7 4.8 fusion.45
  436.6 0.1 dynamic_update_slice.14
  436.7 4.8 fusion.45
  441.5 0.1 dynamic_update_slice.14
  441.6 4.8 fusion.45
  446.5 0.1 dynamic_update_slice.14
  446.6 4.8 fusion.45
  451.5 0.1 dynamic_update_slice.14
  451.6 41.6 %all-reduce.4 = (f32[2048]{0:T(1024)S(1)}, f32[2048]{0:T(1024)S(1)}) all-reduce(f32[2048]{0:T(1024)S(1)} %bitcast.72, f32[2048]{0:T(1024)S(1)} %bitcast.71), channel_id=3, replica_groups=mesh['row'=16,'col'=8] {'col'}, use_global_device_ids=true, to_apply=%region_16.17.clone | all-reduce | flops 4096 | bytes 32768
  493.1 1.2 fusion.25
  (38 shorter events, 0.5 us)
Async XLA Ops:
  7.2 2.9 copy-start.3
  7.2 242.8 %all-reduce.7.cloned.1.call-start = ((), (), s32[]{:S(2)}) async-start(), calls=%async_computation | async-start | bytes 16777216 | tf_op jit(solution)/shard_map/psum | solution.py:49
  91.8 302.8 %all-gather.4.cloned.1.call-start = ((), (), s32[]{:S(2)}) async-start(), calls=%async_computation.1 | async-start | bytes 1179648 | tf_op jit(solution)/shard_map/all_gather | solution.py:55
  329.1 5.7 %copy-start = (f32[8192,256]{1,0:T(8,128)S(1)}, f32[8192,256]{1,0:T(8,128)}, u32[]{:S(2)}) copy-start(f32[8192,256]{1,0:T(8,128)} %all-reduce.7.cloned.1.call-done) | copy-start | bytes 25165828
  341.5 5.5 %copy-start.1 = (bf16[256,8192]{1,0:T(8,128)(2,1)S(1)}, bf16[256,8192]{1,0:T(8,128)(2,1)}, u32[]{:S(2)}) copy-start(bf16[256,8192]{1,0:T(8,128)(2,1)} %param.6) | copy-start | bytes 12582916
  345.7 1.3 copy-start.2
  347.0 21.8 %copy-start.4 = (u32[128]{0:T(128)S(1)}, u32[128]{0:T(128)}, u32[]{:S(2)}) copy-start(u32[128]{0:T(128)} %constant.145) | copy-start | bytes 1540
  349.1 80.3 %all-gather.6.cloned.1.call-start = ((), (), s32[]{:S(2)}) async-start(), calls=%async_computation.2 | async-start | bytes 2228224 | tf_op jit(solution)/shard_map/all_gather | solution.py:57
Sparse Core Ops, SparseCore 0:
  91.9 157.9 all-reduce.6
  349.3 45.3 all-gather.3
  396.9 32.4 all-gather.5
where the time goes:
time: 507 us; the launch traced here: 501 us
  waiting for transfers between devices  206 us (41%)
  blocking collectives  128 us (25%)
  matrix products  70.1 us (14%)
  other arithmetic  66.3 us (13%)
  between operations  17.7 us (3%)
  local copies, waits for them, and re-layouts  13 us (3%)
    psum x1, waiting for transfers between devices, local(): gram = lax.psum(gram_part, ('row', 'col'))  158 us
    psum x1, blocking collectives, local(): lax.psum((jnp.sum(samples, 0, dtype=jnp.float32), jnp.sum(is_ref)), ('row...  68.6 us
    unnamed x1, blocking collectives  41.6 us
    another operation x6, other arithmetic, local(): factor = jnp.linalg.cholesky(square)  34 us
    all_gather x1, waiting for transfers between devices, local(): lax.all_gather(projected, 'row', axis=0, tiled=True)  33.2 us
    another operation x3, other arithmetic, local(): jax.scipy.linalg.solve_triangular(factor, gram.T, lower=True)  19.9 us
    dot_general x4, matrix products, block_sums(): lax.dot_general(block_rows, panel_cols, (((1,), (1,)), ((), ())), preferr...  19.4 us
    dot_general x1, matrix products, local(): square = jnp.dot(gram.T, gram, precision=lax.Precision.HIGHEST)  19.2 us
  transfers between devices with their start and end apart: 3, of which 3 were waited for; matrix products, arithmetic and copies ran while one was open for 2% of the time, Pallas kernels for 0%

commit v1 on v0

v1 whole, which is shorter than its diff:
```python
import functools

import jax
import jax.numpy as jnp
from jax import lax
from jax.experimental import pallas as pl
from jax.experimental.pallas import tpu as pltpu
from jax.sharding import PartitionSpec as P

MESH = pl.DeviceIdType.MESH
F32 = jnp.float32
BF16 = jnp.bfloat16
VMEM = pl.BlockSpec(memory_space=pltpu.VMEM)
HIGHEST = lax.Precision.HIGHEST
LIMIT = 60 * 1024 * 1024

PARTS = ((0, 48, (0, 1, 2)), (48, 48, (1, 2, 0)), (96, 32, (2, 0, 1)))
GATHER = ((0, 32, (2, 1, 0)), (32, 16, (0, 2, 1)), (48, 16, (1, 0, 2)))


def place():
    row, col = lax.axis_index("row"), lax.axis_index("col")
    y, z_lo, core = row // 4, (row // 2) % 2, row % 2
    z_hi, x = col // 4, col % 4
    return (x, y, z_hi * 2 + z_lo), core


def device(at, core):
    x, y, z = at
    return (y * 4 + (z % 2) * 2 + core, (z // 2) * 4 + x)


def moved(at, axis, offset):
    return tuple((c + offset) % 4 if a == axis else c for a, c in enumerate(at))


class Copies:
    def __init__(self, send, recv):
        self.send, self.recv, self.used = send, recv, 0

    def start(self, src, dst, target):
        n = self.used
        self.used += 1
        copy = pltpu.make_async_remote_copy(
            src_ref=src,
            dst_ref=dst,
            send_sem=self.send.at[n],
            recv_sem=self.recv.at[n],
            device_id=target,
            device_id_type=MESH,
        )
        copy.start()
        return copy


def greet(peers):
    barrier = pltpu.get_barrier_semaphore()
    for peer in peers:
        pl.semaphore_signal(barrier, inc=1, device_id=peer, device_id_type=MESH)
    pl.semaphore_wait(barrier, len(peers))


def axis_peers(at, core):
    return [device(moved(at, a, o), core) for a in range(3) for o in (1, 2, 3)]


def pick(axes, at, rows=None):
    index = tuple(at[a] if a in axes else slice(None) for a in range(3))
    return index if rows is None else (*index, rows)


def gram_kernel(
    n_total, x_ref, b_ref, g_ref, s_ref, mean_ref,
    c_ref, local_ref, mhalf, mrecv0, mrecv, daug, gt, half, recv0,
    r1a, r1b, r1c, t1a, t1b, t1c, r2a, r2b, r2c, t2a, t2b, t2c, r3a, r3b, r3c,
    gme, s_half, sr0, sr1, ss1, sr2, ss2, send, recv,
):
    at, core = place()
    x, y, z = at
    other = 1 - core
    copies = Copies(send, recv)
    partner = device(at, other)
    greet([partner, *axis_peers(at, core)])
    n_local, width = x_ref.shape

    @pl.loop(0, width // 256)
    def _(j):
        lanes = pl.ds(pl.multiple_of(j * 256, 256), 256)
        m = jnp.sum(x_ref[:, lanes].astype(F32), 0, keepdims=True) * (1.0 / n_local)
        local_ref[pl.ds(2 * j, 1), :] = m[:, :128]
        local_ref[pl.ds(2 * j + 1, 1), :] = m[:, 128:]

    mine = pl.ds(pl.multiple_of(core * 32, 32), 32)
    theirs = pl.ds(pl.multiple_of(other * 32, 32), 32)
    copy = copies.start(local_ref.at[theirs], mrecv0, partner)

    @pl.loop(0, width // 256)
    def _(j):
        lanes = pl.ds(pl.multiple_of(j * 256, 256), 256)
        rows = local_ref[pl.ds(2 * j, 2), :]
        m = jnp.concatenate([rows[0:1], rows[1:2]], 1)
        c_ref[:, lanes] = (x_ref[:, lanes].astype(F32) - m).astype(BF16)

    first = jnp.zeros((n_local, b_ref.shape[1]), F32)
    pieces = 4
    deep = width // pieces
    copy.wait()
    mhalf[0] = local_ref[mine, :] + mrecv0[...]
    for a in range(3):
        waits = [copies.start(mhalf.at[a], mrecv.at[a, o - 1], device(moved(at, a, o), core)) for o in (1, 2, 3)]
        first += jnp.dot(
            c_ref[:, a * deep : (a + 1) * deep], b_ref[a * deep : (a + 1) * deep, :], preferred_element_type=F32
        )
        for w in waits:
            w.wait()
        mhalf[a + 1] = mhalf[a] + mrecv[a, 0] + mrecv[a, 1] + mrecv[a, 2]
    mhalf[4] = mhalf[3] * (1.0 / 128.0)
    mean_ref[mine, :] = mhalf[4]
    copy = copies.start(mhalf.at[4], mean_ref.at[mine], partner)
    first += jnp.dot(c_ref[:, 3 * deep :], b_ref[3 * deep :, :], preferred_element_type=F32)
    first_t = first.T.astype(BF16)
    copy.wait()

    ids = lax.broadcasted_iota(jnp.int32, (16, 128), 0)

    @pl.loop(0, width // 128)
    def _(j):
        delta = local_ref[pl.ds(j, 1), :] - mean_ref[pl.ds(j, 1), :]
        high = delta.astype(BF16).astype(F32)
        low = delta - high
        tile = jnp.where(ids == 1, low, jnp.where((ids == 0) | (ids == 2), high, 0.0))
        daug[:, pl.ds(pl.multiple_of(j * 128, 128), 128)] = tile.astype(BF16)

    tau = jnp.dot(daug[...], b_ref[...], preferred_element_type=F32)
    tau = (tau[0:1] + tau[1:2]) * float(n_local)
    t_high = tau.astype(BF16).astype(F32)
    ids = lax.broadcasted_iota(jnp.int32, (16, 256), 0)
    taug = jnp.where(ids == 2, tau - t_high, jnp.where(ids < 2, t_high, 0.0))
    taug_t = taug.T.astype(BF16)

    @pl.loop(0, width // 256)
    def _(j):
        lanes = pl.ds(pl.multiple_of(j * 256, 256), 256)
        block = jnp.dot(first_t, c_ref[:, lanes], preferred_element_type=F32)
        block += jnp.dot(taug_t, daug[:, lanes], preferred_element_type=F32)
        block = block.astype(BF16)
        bx, by, bz = j // 8, (j // 2) % 4, (j % 2) * 2
        gt[bx, by, bz] = block[:, :128]
        gt[bx, by, bz + 1] = block[:, 128:]

    near = pl.ds(pl.multiple_of(core * 128, 128), 128)
    far = pl.ds(pl.multiple_of(other * 128, 128), 128)
    copies.start(gt.at[:, :, :, far, :], recv0, partner).wait()

    @pl.loop(0, 64)
    def _(j):
        bx, by, bz = j // 16, (j // 4) % 4, j % 4
        half[bx, by, bz] = (gt[bx, by, bz, near, :].astype(F32) + recv0[bx, by, bz].astype(F32)).astype(BF16)

    parts = list(zip(PARTS, (r1a, r1b, r1c), (t1a, t1b, t1c), (r2a, r2b, r2c), (t2a, t2b, t2c), (r3a, r3b, r3c)))
    waits = []
    for (start, size, order), r1, _, _, _, _ in parts:
        rows = slice(start, start + size)
        for o in (1, 2, 3):
            to = moved(at, order[0], o)
            waits.append(copies.start(half.at[pick(order[:1], to, rows)], r1.at[o - 1], device(to, core)))
    for w in waits:
        w.wait()
    waits = []
    for (start, size, order), r1, t1, r2, _, _ in parts:
        rows = slice(start, start + size)
        own = half.at[pick(order[:1], at, rows)]

        @pl.loop(0, 16)
        def _(j):
            u, v = j // 4, j % 4
            t1[u, v] = (own[u, v].astype(F32) + r1[0, u, v].astype(F32)) + (
                r1[1, u, v].astype(F32) + r1[2, u, v].astype(F32)
            )

        left = [a for a in range(3) if a != order[0]]
        for o in (1, 2, 3):
            to = moved(at, order[1], o)
            index = (to[order[1]],) if left[0] == order[1] else (slice(None), to[order[1]])
            waits.append(copies.start(t1.at[index], r2.at[o - 1], device(to, core)))
    for w in waits:
        w.wait()
    waits = []
    for (start, size, order), _, t1, r2, t2, r3 in parts:
        left = [a for a in range(3) if a != order[0]]
        first_left = left[0] == order[1]
        for k in range(4):
            own = t1[at[order[1]], k] if first_left else t1[k, at[order[1]]]
            t2[k] = (own + r2[0, k]) + (r2[1, k] + r2[2, k])
        for o in (1, 2, 3):
            to = moved(at, order[2], o)
            waits.append(copies.start(t2.at[to[order[2]]], r3.at[o - 1], device(to, core)))
    for w in waits:
        w.wait()
    for (start, size, order), _, _, _, t2, r3 in parts:
        total = (t2[at[order[2]]] + r3[0]) + (r3[1] + r3[2])
        gme[start : start + size, :] = total * (1.0 / n_total)
    g_ref[near, :] = gme[...]
    copies.start(gme, g_ref.at[near], partner).wait()

    square = lax.dot_general(
        gme[...], g_ref[...], (((1,), (1,)), ((), ())), precision=HIGHEST, preferred_element_type=F32
    )
    s_half[0] = square[:, :128]
    s_half[1] = square[:, 128:]
    waits = []
    for o in (1, 2, 3):
        to = moved(at, 0, o)
        rows = pl.ds(pl.multiple_of(to[0] * 32, 32), 32)
        waits.append(copies.start(s_half.at[:, rows, :], sr0.at[o - 1], device(to, core)))
    for w in waits:
        w.wait()
    ss1[...] = (s_half[:, pl.ds(pl.multiple_of(x * 32, 32), 32), :] + sr0[0]) + (sr0[1] + sr0[2])
    waits = []
    for o in (1, 2, 3):
        to = moved(at, 1, o)
        rows = pl.ds(pl.multiple_of(to[1] * 8, 8), 8)
        waits.append(copies.start(ss1.at[:, rows, :], sr1.at[o - 1], device(to, core)))
    for w in waits:
        w.wait()
    ss2[...] = (ss1[:, pl.ds(pl.multiple_of(y * 8, 8), 8), :] + sr1[0]) + (sr1[1] + sr1[2])
    waits = []
    for o in (1, 2, 3):
        waits.append(copies.start(ss2, sr2.at[z], device(moved(at, 2, o), core)))
    sr2[z] = ss2[...]
    for w in waits:
        w.wait()
    base = pl.multiple_of(core * 128 + x * 32 + y * 8, 8)
    s_ref[:, pl.ds(base, 8), :] = (sr2[0] + sr2[1]) + (sr2[2] + sr2[3])
    for axis, rows in (
        (1, pl.ds(base, 8)),
        (0, pl.ds(pl.multiple_of(core * 128 + x * 32, 32), 32)),
    ):
        view = s_ref.at[:, rows, :]
        waits = [copies.start(view, view, device(moved(at, axis, o), core)) for o in (1, 2, 3)]
        for w in waits:
            w.wait()
    view = s_ref.at[:, near, :]
    copies.start(view, view, partner).wait()


def gram_and_square(samples, basis_start, n_total):
    scratch = [
        pltpu.VMEM((256, 8192), BF16),
        pltpu.VMEM((64, 128), F32),
        pltpu.VMEM((5, 32, 128), F32),
        pltpu.VMEM((32, 128), F32),
        pltpu.VMEM((3, 3, 32, 128), F32),
        pltpu.VMEM((16, 8192), BF16),
        pltpu.VMEM((4, 4, 4, 256, 128), BF16),
        pltpu.VMEM((4, 4, 4, 128, 128), BF16),
        pltpu.VMEM((4, 4, 4, 128, 128), BF16),
        *[pltpu.VMEM((3, 4, 4, size, 128), BF16) for _, size, _ in PARTS],
        *[pltpu.VMEM((4, 4, size, 128), F32) for _, size, _ in PARTS],
        *[pltpu.VMEM((3, 4, size, 128), F32) for _, size, _ in PARTS],
        *[pltpu.VMEM((4, size, 128), F32) for _, size, _ in PARTS],
        *[pltpu.VMEM((3, size, 128), F32) for _, size, _ in PARTS],
        pltpu.VMEM((128, 128), F32),
        pltpu.VMEM((2, 128, 128), F32),
        pltpu.VMEM((3, 2, 32, 128), F32),
        pltpu.VMEM((3, 2, 8, 128), F32),
        pltpu.VMEM((2, 32, 128), F32),
        pltpu.VMEM((4, 2, 8, 128), F32),
        pltpu.VMEM((2, 8, 128), F32),
        pltpu.SemaphoreType.DMA((56,)),
        pltpu.SemaphoreType.DMA((56,)),
    ]
    return pl.pallas_call(
        functools.partial(gram_kernel, n_total),
        out_shape=(
            jax.ShapeDtypeStruct((256, 128), F32),
            jax.ShapeDtypeStruct((2, 256, 128), F32),
            jax.ShapeDtypeStruct((64, 128), F32),
        ),
        in_specs=[VMEM, VMEM],
        out_specs=(VMEM, VMEM, VMEM),
        scratch_shapes=scratch,
        compiler_params=pltpu.CompilerParams(collective_id=0, has_side_effects=True, vmem_limit_bytes=LIMIT),
        name="gram",
    )(samples, basis_start)


def basis_kernel(g_ref, inv_ref, out_ref, send, recv):
    at, core = place()
    copies = Copies(send, recv)
    partner = device(at, 1 - core)
    greet([partner, *axis_peers(at, core)])
    block = lax.dot_general(
        g_ref[...], inv_ref[...], (((0,), (1,)), ((), ())), precision=HIGHEST, preferred_element_type=F32
    ).astype(BF16)
    out_ref[at[0], at[1], at[2], core] = jnp.where(core == 0, block[:64], block[64:])
    for step in range(3):
        waits = []
        for start, size, order in GATHER:
            fixed = order[step:]
            view = out_ref.at[(*pick(fixed, at), core, slice(start, start + size))]
            for o in (1, 2, 3):
                waits.append(copies.start(view, view, device(moved(at, order[step], o), core)))
        for w in waits:
            w.wait()
    waits = []
    for o in range(4):
        bx = (at[0] + o) % 4
        view = out_ref.at[bx, :, :, core]
        waits.append(copies.start(view, view, partner))
    for w in waits:
        w.wait()


def gather_basis(g, inverse):
    out = pl.pallas_call(
        basis_kernel,
        out_shape=jax.ShapeDtypeStruct((4, 4, 4, 2, 64, 256), BF16),
        in_specs=[VMEM, VMEM],
        out_specs=VMEM,
        scratch_shapes=[pltpu.SemaphoreType.DMA((31,)), pltpu.SemaphoreType.DMA((31,))],
        compiler_params=pltpu.CompilerParams(collective_id=1, has_side_effects=True, vmem_limit_bytes=LIMIT),
        name="basis",
    )(g, inverse)
    return out.reshape(8192, 256)


def proof_kernel(
    n_total, width_ref, p_ref, label_ref, out_ref,
    rowp, colp, negrow, acc_all, acc_ref, pay, got, send, recv,
):
    at, core = place()
    x, y, z = at
    z_lo, z_hi = z % 2, z // 2
    copies = Copies(send, recv)
    partner = device(at, 1 - core)
    me_row, me_col = lax.axis_index("row"), lax.axis_index("col")
    rows = [((x + o) % 4, (z_hi + h) % 2) for h in (0, 1) for o in (0, 1, 2, 3)]
    cols = [((y + o) % 4, (z_lo + h) % 2) for h in (0, 1) for o in (0, 1, 2, 3)]
    row_devices = [device((rx, y, rh * 2 + z_lo), core) for rx, rh in rows]
    col_devices = [device((x, cy, z_hi * 2 + cl), core) for cy, cl in cols]
    greet([partner, *row_devices[1:], *col_devices[1:]])

    is_ref = (label_ref[...] == 0).astype(F32)
    mine_row, mine_col = rowp.at[me_col], colp.at[me_row]
    tail = jnp.broadcast_to(is_ref, (16, 256)).astype(BF16)
    mine_row[0:256, :] = p_ref[...]
    mine_row[256:272, :] = tail
    mine_col[0:256, :] = p_ref[...]
    mine_col[256:272, :] = tail
    row_waits = [copies.start(mine_row, mine_row, d) for d in row_devices[1:]]
    col_waits = [copies.start(mine_col, mine_col, d) for d in col_devices[1:]]
    core_waits = [copies.start(mine_col, mine_col, partner)]
    for (cy, cl), o, h, w in zip(cols[1:], (1, 2, 3, 0, 1, 2, 3), (0, 0, 0, 1, 1, 1, 1), col_waits):
        w.wait()
        slot = ((y + 4 - o) % 4) * 4 + ((z_lo + h) % 2) * 2 + core
        view = colp.at[slot]
        core_waits.append(copies.start(view, view, partner))
    for w in row_waits:
        w.wait()

    scale = 1.4426950408889634 / (128.0 * jnp.exp2(jnp.full((1, 256), width_ref[0], jnp.int32).astype(F32)))
    ones = jnp.ones((8, 256), F32)
    for q in range(8):
        p = rowp[q, 0:256, :].astype(F32)
        norm = lax.dot_general(ones, p * p, (((1,), (1,)), ((), ())), precision=HIGHEST, preferred_element_type=F32)
        negrow[q] = norm * -0.5
        acc_all[q] = jnp.zeros((8, 256), F32)
        acc_ref[q] = jnp.zeros((8, 256), F32)
    for w in core_waits:
        w.wait()

    def column(r, count):
        block = colp[r, 0:256, :]
        p = block.astype(F32)
        half_norm = jnp.sum(p * p, 1, keepdims=True) * -0.5
        mark_row = colp[r, 256:272, :].astype(F32)[0:1]
        mark = jnp.concatenate(
            [jnp.broadcast_to(mark_row[:, :128], (128, 128)).T, jnp.broadcast_to(mark_row[:, 128:], (128, 128)).T], 0
        )
        mark = jnp.concatenate([mark, mark], 1)

        def row_block(q, carry):
            inner = lax.dot_general(
                block, rowp[q, 0:256, :], (((1,), (1,)), ((), ())), preferred_element_type=F32
            )
            value = jnp.exp2(((inner + half_norm) + negrow[q][0:1]) * scale)
            acc_all[q] += jnp.sum(value.reshape(32, 8, 256), 0)
            acc_ref[q] += jnp.sum((value * mark).reshape(32, 8, 256), 0)
            return carry

        lax.fori_loop(0, 8, row_block, 0)
        return count + mark_row

    count = lax.fori_loop(0, 16, column, jnp.zeros((1, 256), F32))
    ids = lax.broadcasted_iota(jnp.int32, (8, 256), 0)
    for q in range(8):
        total = jnp.sum(acc_all[q], 0, keepdims=True)
        refs = jnp.sum(acc_ref[q], 0, keepdims=True)
        pay[q] = jnp.where(ids == 0, total, jnp.where(ids == 1, refs, count))
    waits = []
    for (rx, rh), d in zip(rows[1:], row_devices[1:]):
        waits.append(copies.start(pay.at[rh * 4 + rx], got.at[me_col], d))
    got[me_col] = pay[me_col]
    for w in waits:
        w.wait()
    total = jnp.sum(got[...], 0)
    row_sums, ref_sums = total[0:1], total[1:2]
    n_ref = jnp.sum(total[2:3], 1, keepdims=True)
    n_cur = n_total - n_ref
    proof = (ref_sums / n_ref - (row_sums - ref_sums) / n_cur) / (row_sums / n_total)
    out_ref[...] = jnp.broadcast_to(proof, (8, 256))


def proof_values(projected, labels, width_index, n_total):
    out = pl.pallas_call(
        functools.partial(proof_kernel, n_total),
        out_shape=jax.ShapeDtypeStruct((8, 256), F32),
        in_specs=[pl.BlockSpec(memory_space=pltpu.SMEM), VMEM, VMEM],
        out_specs=VMEM,
        scratch_shapes=[
            pltpu.VMEM((8, 272, 256), BF16),
            pltpu.VMEM((16, 272, 256), BF16),
            pltpu.VMEM((8, 8, 256), F32),
            pltpu.VMEM((8, 8, 256), F32),
            pltpu.VMEM((8, 8, 256), F32),
            pltpu.VMEM((8, 8, 256), F32),
            pltpu.VMEM((8, 8, 256), F32),
            pltpu.SemaphoreType.DMA((29,)),
            pltpu.SemaphoreType.DMA((29,)),
        ],
        compiler_params=pltpu.CompilerParams(collective_id=2, has_side_effects=True, vmem_limit_bytes=LIMIT),
        name="proof",
    )(width_index.reshape(1), projected, labels.reshape(1, 256))
    return out[0]


def local(n_total, samples, labels, basis_start, width_index):
    g, square, mean = gram_and_square(samples, basis_start, n_total)
    square = jnp.concatenate([square[0], square[1]], 1)
    factor = jnp.linalg.cholesky(square)
    inverse = jax.scipy.linalg.solve_triangular(factor, jnp.eye(256, dtype=F32), lower=True)
    basis = gather_basis(g, inverse)
    centred = (samples - mean.reshape(1, 8192)).astype(BF16)
    projected = jnp.dot(centred, basis, preferred_element_type=F32).astype(BF16)
    proof = proof_values(projected, labels, width_index, n_total)
    return projected, proof, basis


def solution(mesh):
    n_total = float(256 * mesh.size)
    placed = (P(("row", "col"), None), P(("row", "col")), P(), P())
    return jax.shard_map(
        functools.partial(local, n_total),
        mesh=mesh,
        in_specs=placed,
        out_specs=(P(("row", "col"), None), P(("row", "col")), P()),
        check_vma=False,
    )
```

time: 507 us -> 266 us (0.52); the launches traced: 501 us -> 266 us
  waiting for transfers between devices: 206 us -> 0 us
  Pallas kernels: 0 us -> 191 us
  blocking collectives: 128 us -> 0 us
  matrix products: 70.1 us -> 6.69 us
  between operations: 17.7 us -> 2.76 us
  other arithmetic: 66.3 us -> 54.7 us
    pallas_call x0 -> x3, Pallas kernels: none -> 191 us  [the longest x1 83.5 us: gram_and_square(): pl.pallas_call(functools.partial(gram_kernel, n_total), out_shape=(jax.Sh...]
    psum x1 -> x0, waiting for transfers between devices: 158 us -> none  [local(): gram = lax.psum(gram_part, ('row', 'col'))]
    psum x1 -> x0, blocking collectives: 68.6 us -> none  [local(): lax.psum((jnp.sum(samples, 0, dtype=jnp.float32), jnp.sum(is_ref)), ('row...]
    dot_general x7 -> x1, matrix products: 53.2 us -> 5.39 us  [local(): projected = jnp.dot(centred, basis, preferred_element_type=F32).astype(BF16)]
    all_gather x2 -> x0, waiting for transfers between devices: 47.5 us -> none  [the longest x1 33.2 us: local(): lax.all_gather(projected, 'row', axis=0, tiled=True)]
    unnamed x1 -> x0, blocking collectives: 41.6 us -> none
    all_gather x1 -> x0, blocking collectives: 17.6 us -> none  [local(): lax.all_gather(is_ref.astype(jnp.bfloat16), 'row', axis=0, tiled=True)]
    another operation x3, matrix products: 16.5 us -> 0.83 us  [local(): jax.scipy.linalg.solve_triangular(factor, jnp.eye(256, dtype=F32), lower=...]
  transfers between devices with their start and end apart: 3 -> 0, of which waited for: 3 -> 0; matrix products, arithmetic and copies ran while one was open for 2% -> 0% of each run, Pallas kernels for 0% -> 0%
where the time goes in v1:
time: 266 us
  Pallas kernels  191 us (72%)
  other arithmetic  54.7 us (21%)
  local copies, waits for them, and re-layouts  11 us (4%)
  matrix products  6.69 us (3%)
  between operations  2.76 us (1%)
    pallas_call x1, Pallas kernels, gram_and_square(): pl.pallas_call(functools.partial(gram_kernel, n_total), out_shape=(jax.Sh...  83.5 us
    pallas_call x1, Pallas kernels, proof_values(): pl.pallas_call(functools.partial(proof_kernel, n_total), out_shape=jax.Sh...  76.7 us
    another operation x6, other arithmetic, local(): factor = jnp.linalg.cholesky(square)  34 us
    pallas_call x1, Pallas kernels, gather_basis(): pl.pallas_call(basis_kernel, out_shape=jax.ShapeDtypeStruct((4, 4, 4, 2,...  30.3 us
    another operation x4, other arithmetic, local(): jax.scipy.linalg.solve_triangular(factor, jnp.eye(256, dtype=F32), lower=...  20.6 us
    dot_general x1, matrix products, local(): projected = jnp.dot(centred, basis, preferred_element_type=F32).astype(BF16)  5.39 us

profile of v1, /device:TPU:0, one launch (start us, length us, event | category | flops | bytes accessed | tf_op | source)
XLA Modules:
  0.0 265.7 jit_solution(9908717589629412155)
XLA Ops:
  1.3 0.1 triangular_solve.63
  1.4 83.5 %gram.1 = (f32[256,128]{1,0:T(8,128)}, f32[2,256,128]{2,1,0:T(8,128)}, f32[64,128]{1,0:T(8,128)}) custom-call(bf16[256,8192]{1,0:T(8,128)(2,1)} %x_ref.1, bf16[8192,256]{1,0:T(8,128)(2,1)} %b_ref.1), custom_call_target="tpu_custom_call" | custom-call | tf_op jit(solution)/shard_map/gram/pallas_call | solution.py:273
  84.9 1.1 copy.7
  86.0 0.1 copy.9
  86.2 11.7 %cholesky.50 = f32[128,128]{1,0:T(8,128)S(1)} custom-call(f32[128,128]{1,0:T(8,128)S(1)} %cholesky.118), custom_call_target="Cholesky" | custom-call | tf_op jit(solution)/shard_map/jit(cholesky)/cholesky | solution.py:441
  98.0 9.8 %custom-call.15 = f32[1,128,128]{1,2,0:T(8,128)S(1)} custom-call(f32[1,128,128]{2,1,0:T(8,128)S(1)} %get-tuple-element.32), custom_call_target="InvertDiagBlocksLowerTriangular" | custom-call | tf_op jit(solution)/shard_map/jit(cholesky)/cholesky | solution.py:441
  107.8 0.0 copy-start
  107.8 0.2 constant_dynamic-update-slice_fusion.1
  108.1 0.3 convolution_subtract_fusion.1
  108.3 11.7 %cholesky.105 = f32[128,128]{1,0:T(8,128)S(1)} custom-call(f32[128,128]{1,0:T(8,128)S(1)} %convolution_subtract_fusion.1), custom_call_target="Cholesky" | custom-call | tf_op jit(solution)/shard_map/jit(cholesky)/cholesky | solution.py:441
  120.1 0.6 compare_reduce_fusion
  122.1 4.0 %while.1 = (s32[]{:T(128)}, f32[256,256]{1,0:T(8,128)S(1)}, s32[2,2]{1,0:T(2,128)S(1)}, f32[2,128,128]{2,1,0:T(8,128)S(1)}, s32[]{:T(128)}) while((s32[]{:T(128)}, f32[256,256]{1,0:T(8,128)S(1)}, s32[2,2]{1,0:T(2,128)S(1)}, f32[2,128,128]{2,1,0:T(8,128)S(1)}, s32[]{:T(128)}) %tuple.28), condition=%wide.while_cond, body=%wide.while_body.sunk | while | flops 2 | bytes 131189 | solution.py:442
  122.1 0.6 fusion.18
  122.7 1.4 bitcast_dynamic-update-slice_fusion.2
  124.1 0.6 fusion.18
  124.7 1.4 bitcast_dynamic-update-slice_fusion.2
  126.1 19.9 %custom-call.16 = f32[2,128,128]{1,2,0:T(8,128)S(1)} custom-call(f32[2,128,128]{2,1,0:T(8,128)S(1)} %get-tuple-element.16), custom_call_target="InvertDiagBlocksLowerTriangular" | custom-call | tf_op jit(solution)/shard_map/jit(_solve_triangular)/triangular_solve | solution.py:442
  146.0 0.3 fusion.4
  146.2 0.3 convolution_subtract_fusion
  146.5 0.3 fusion.7
  146.8 0.7 pad_maximum_fusion.1.inv_ref
  147.5 30.3 %basis.1 = bf16[4,4,4,2,64,256]{5,4,3,2,1,0:T(8,128)(2,1)} custom-call(f32[256,128]{1,0:T(8,128)} %get-tuple-element.7.g_ref, f32[256,256]{1,0:T(8,128)} %pad_maximum_fusion.1.inv_ref), custom_call_target="tpu_custom_call" | custom-call | tf_op jit(solution)/shard_map/basis/pallas_call | solution.py:316
  177.8 0.0 copy-done
  177.8 5.4 %fusion.2.p_ref = bf16[256,256]{1,0:T(8,128)(2,1)} fusion(bf16[8192,256]{1,0:T(8,128)(2,1)} %bitcast.42, bf16[256,8192]{1,0:T(8,128)(2,1)} %x_ref.1, f32[8192]{0:T(1024)S(1)} %bitcast.46), kind=kOutput, calls=%fused_computation.5 | convolution fusion | flops 1080098816 | bytes 8552448 | tf_op jit(solution)/shard_map/dot_general | solution.py:445
  183.2 76.7 %proof.1 = f32[8,256]{1,0:T(8,128)} custom-call(s32[1]{0:T(128)} %bitcast.41.width_ref, bf16[256,256]{1,0:T(8,128)(2,1)} %fusion.2.p_ref, s32[1,256]{1,0:T(1,128)} %bitcast.44), custom_call_target="tpu_custom_call" | custom-call | tf_op jit(solution)/shard_map/proof/pallas_call | solution.py:416
  260.0 1.3 slice.59
  261.2 4.5 %copy.24 = bf16[8192,256]{1,0:T(8,128)(2,1)} copy(bf16[8192,256]{1,0:T(8,128)(2,1)} %bitcast.43) | data formatting | bytes 8388608
  (13 shorter events, 0.2 us)
Async XLA Ops:
  107.8 70.0 %copy-start = (f32[64,128]{1,0:T(8,128)S(1)}, f32[64,128]{1,0:T(8,128)}, u32[]{:S(2)}) copy-start(f32[64,128]{1,0:T(8,128)} %get-tuple-element.6) | copy-start | bytes 98308

commit v2 on v1

--- a/solution.py
+++ b/solution.py
@@ -285,13 +285,76 @@
     )(samples, basis_start)
 
 
-def basis_kernel(g_ref, inv_ref, out_ref, send, recv):
+def small_inverse(t):
+    sub = lax.broadcasted_iota(jnp.int32, (8, 128), 0)
+    t = list(t)
+    for s in range(4):
+        rows = [jnp.broadcast_to(t[s][i : i + 1, :], (8, 128)) for i in range(8)]
+        e = [[jnp.broadcast_to(rows[i][:, 8 * s + j : 8 * s + j + 1], (8, 128)) for j in range(i + 1)] for i in range(8)]
+        inv, low = [], [[None] * 8 for _ in range(8)]
+        for j in range(8):
+            inv.append(1.0 / e[j][j])
+            for i in range(j + 1, 8):
+                low[i][j] = e[i][j] * inv[j]
+            for i in range(j + 1, 8):
+                for m in range(j + 1, i + 1):
+                    e[i][m] = e[i][m] - low[i][j] * e[m][j]
+        w = []
+        for i in range(8):
+            v = rows[i]
+            for j in range(i):
+                v = v - low[i][j] * w[j]
+            w.append(v)
+        for b in range(s + 1, 4):
+            f = []
+            for j in range(8):
+                v = jnp.broadcast_to(t[b][:, 8 * s + j : 8 * s + j + 1], (8, 128))
+                for k in range(j):
+                    v = v - f[k] * e[j][k]
+                f.append(v * inv[j])
+            for j in range(8):
+                t[b] = t[b] - f[j] * w[j]
+        out = w[0] * lax.rsqrt(e[0][0])
+        for i in range(1, 8):
+            out = jnp.where(sub == i, w[i] * lax.rsqrt(e[i][i]), out)
+        t[s] = out
+    return t
+
+
+def inverse_factor(s_ref, m_ref):
+    r = lax.broadcasted_iota(jnp.int32, (256, 256), 0)
+    c = lax.broadcasted_iota(jnp.int32, (256, 256), 1)
+    m_ref[:, 0:128] = s_ref[0]
+    m_ref[:, 128:256] = s_ref[1]
+    m_ref[:, 256:512] = (r == c).astype(F32)
+    lane = lax.broadcasted_iota(jnp.int32, (32, 128), 1)
+    unit = (lane == lax.broadcasted_iota(jnp.int32, (32, 128), 0) + 32).astype(F32)
+    wide = lax.broadcasted_iota(jnp.int32, (32, 256), 1)
+
+    def panel(b, carry):
+        rows = pl.ds(pl.multiple_of(b * 32, 32), 32)
+        tile = m_ref[rows, pl.ds(pl.multiple_of((b // 4) * 128, 128), 128)]
+        tile = pltpu.roll(tile, (4 - b % 4) % 4 * 32, 1)
+        tile = jnp.where(lane < 32, tile, unit)
+        t = small_inverse([tile[8 * i : 8 * i + 8] for i in range(4)])
+        inv = jnp.concatenate(t, 0)[:, 32:64]
+        w = jnp.dot(inv, m_ref[rows, :], precision=HIGHEST, preferred_element_type=F32)
+        left = jnp.where(wide >= (b + 1) * 32, w[:, :256], 0.0)
+        m_ref[...] -= lax.dot_general(left, w, (((0,), (0,)), ((), ())), precision=HIGHEST, preferred_element_type=F32)
+        m_ref[rows, :] = w
+        return carry
+
+    lax.fori_loop(0, 8, panel, 0)
+
+
+def basis_kernel(g_ref, s_ref, out_ref, m_ref, send, recv):
     at, core = place()
     copies = Copies(send, recv)
     partner = device(at, 1 - core)
     greet([partner, *axis_peers(at, core)])
+    inverse_factor(s_ref, m_ref)
     block = lax.dot_general(
-        g_ref[...], inv_ref[...], (((0,), (1,)), ((), ())), precision=HIGHEST, preferred_element_type=F32
+        g_ref[...], m_ref[:, 256:512], (((0,), (1,)), ((), ())), precision=HIGHEST, preferred_element_type=F32
     ).astype(BF16)
     out_ref[at[0], at[1], at[2], core] = jnp.where(core == 0, block[:64], block[64:])
     for step in range(3):
@@ -312,16 +375,16 @@
         w.wait()
 
 
-def gather_basis(g, inverse):
+def gather_basis(g, square):
     out = pl.pallas_call(
         basis_kernel,
         out_shape=jax.ShapeDtypeStruct((4, 4, 4, 2, 64, 256), BF16),
         in_specs=[VMEM, VMEM],
         out_specs=VMEM,
-        scratch_shapes=[pltpu.SemaphoreType.DMA((31,)), pltpu.SemaphoreType.DMA((31,))],
+        scratch_shapes=[pltpu.VMEM((256, 512), F32), pltpu.SemaphoreType.DMA((31,)), pltpu.SemaphoreType.DMA((31,))],
         compiler_params=pltpu.CompilerParams(collective_id=1, has_side_effects=True, vmem_limit_bytes=LIMIT),
         name="basis",
-    )(g, inverse)
+    )(g, square)
     return out.reshape(8192, 256)
 
 
@@ -437,10 +500,7 @@
 
 def local(n_total, samples, labels, basis_start, width_index):
     g, square, mean = gram_and_square(samples, basis_start, n_total)
-    square = jnp.concatenate([square[0], square[1]], 1)
-    factor = jnp.linalg.cholesky(square)
-    inverse = jax.scipy.linalg.solve_triangular(factor, jnp.eye(256, dtype=F32), lower=True)
-    basis = gather_basis(g, inverse)
+    basis = gather_basis(g, square)
     centred = (samples - mean.reshape(1, 8192)).astype(BF16)
     projected = jnp.dot(centred, basis, preferred_element_type=F32).astype(BF16)
     proof = proof_values(projected, labels, width_index, n_total)

time: 266 us -> 217 us (0.82)
  other arithmetic: 54.7 us -> 0 us
  Pallas kernels: 191 us -> 205 us
  local copies, waits for them, and re-layouts: 11 us -> 5.73 us
    another operation x10 -> x0, other arithmetic: 54.6 us -> none  [the longest x6 34 us: local(): factor = jnp.linalg.cholesky(square)]
    pallas_call x1, Pallas kernels: 30.3 us -> 44.3 us  [gather_basis(): pl.pallas_call(basis_kernel, out_shape=jax.ShapeDtypeStruct((4, 4, 4, 2,...]
    another operation x9 -> x0, local copies, waits for them, and re-layouts: 4.05 us -> none
where the time goes in v2:
time: 217 us
  Pallas kernels  205 us (94%)
  local copies, waits for them, and re-layouts  5.73 us (3%)
  matrix products  5.38 us (2%)
    pallas_call x1, Pallas kernels, gram_and_square(): pl.pallas_call(functools.partial(gram_kernel, n_total), out_shape=(jax.Sh...  83.5 us
    pallas_call x1, Pallas kernels, proof_values(): pl.pallas_call(functools.partial(proof_kernel, n_total), out_shape=jax.Sh...  76.7 us
    pallas_call x1, Pallas kernels, gather_basis(): pl.pallas_call(basis_kernel, out_shape=jax.ShapeDtypeStruct((4, 4, 4, 2,...  44.3 us
    dot_general x1, matrix products, local(): projected = jnp.dot(centred, basis, preferred_element_type=F32).astype(BF16)  5.38 us
    unnamed x3, local copies, waits for them, and re-layouts  4.47 us

profile of v2, /device:TPU:0, one launch (start us, length us, event | category | flops | bytes accessed | tf_op | source)
XLA Modules:
  0.0 217.0 jit_solution(5208265462185365997)
XLA Ops:
  1.3 83.5 %gram.1 = (f32[256,128]{1,0:T(8,128)}, f32[2,256,128]{2,1,0:T(8,128)}, f32[64,128]{1,0:T(8,128)}) custom-call(bf16[256,8192]{1,0:T(8,128)(2,1)} %x_ref.1, bf16[8192,256]{1,0:T(8,128)(2,1)} %b_ref.1), custom_call_target="tpu_custom_call" | custom-call | tf_op jit(solution)/shard_map/gram/pallas_call | solution.py:273
  84.8 0.0 copy-start
  84.8 44.3 %basis.1 = bf16[4,4,4,2,64,256]{5,4,3,2,1,0:T(8,128)(2,1)} custom-call(f32[256,128]{1,0:T(8,128)} %get-tuple-element.7.g_ref, f32[2,256,128]{2,1,0:T(8,128)} %get-tuple-element.8.s_ref), custom_call_target="tpu_custom_call" | custom-call | tf_op jit(solution)/shard_map/basis/pallas_call | solution.py:379
  129.2 0.0 copy-done
  129.2 5.4 %fusion.2.p_ref = bf16[256,256]{1,0:T(8,128)(2,1)} fusion(bf16[8192,256]{1,0:T(8,128)(2,1)} %bitcast.7, bf16[256,8192]{1,0:T(8,128)(2,1)} %x_ref.1, f32[8192]{0:T(1024)S(1)} %bitcast.11), kind=kOutput, calls=%fused_computation.3 | convolution fusion | flops 1080098816 | bytes 8552448 | tf_op jit(solution)/shard_map/dot_general | solution.py:505
  134.5 76.7 %proof.1 = f32[8,256]{1,0:T(8,128)} custom-call(s32[1]{0:T(128)} %bitcast.6.width_ref, bf16[256,256]{1,0:T(8,128)(2,1)} %fusion.2.p_ref, s32[1,256]{1,0:T(1,128)} %bitcast.9), custom_call_target="tpu_custom_call" | custom-call | tf_op jit(solution)/shard_map/proof/pallas_call | solution.py:479
  211.3 1.3 slice.3
  212.6 4.5 %copy.9 = bf16[8192,256]{1,0:T(8,128)(2,1)} copy(bf16[8192,256]{1,0:T(8,128)(2,1)} %bitcast.8) | data formatting | bytes 8388608
Async XLA Ops:
  84.8 44.4 %copy-start = (f32[64,128]{1,0:T(8,128)S(1)}, f32[64,128]{1,0:T(8,128)}, u32[]{:S(2)}) copy-start(f32[64,128]{1,0:T(8,128)} %get-tuple-element.6) | copy-start | bytes 98308

commit v3 on v2

--- a/solution.py
+++ b/solution.py
@@ -70,8 +70,8 @@
 
 
 def gram_kernel(
-    n_total, x_ref, b_ref, g_ref, s_ref, mean_ref,
-    c_ref, local_ref, mhalf, mrecv0, mrecv, daug, gt, half, recv0,
+    n_total, x_ref, b_ref, label_ref, g_ref, s_ref, mean_ref, count_ref,
+    c_ref, local_ref, count, crecv, mhalf, mrecv0, mrecv, daug, gt, half, recv0,
     r1a, r1b, r1c, t1a, t1b, t1c, r2a, r2b, r2c, t2a, t2b, t2c, r3a, r3b, r3c,
     gme, s_half, sr0, sr1, ss1, sr2, ss2, send, recv,
 ):
@@ -93,6 +93,9 @@
     mine = pl.ds(pl.multiple_of(core * 32, 32), 32)
     theirs = pl.ds(pl.multiple_of(other * 32, 32), 32)
     copy = copies.start(local_ref.at[theirs], mrecv0, partner)
+    is_ref = (label_ref[...] == 0).astype(F32)
+    count[...] = jnp.broadcast_to(jnp.sum(is_ref, 1, keepdims=True), (8, 128))
+    copy_count = copies.start(count, crecv, partner)
 
     @pl.loop(0, width // 256)
     def _(j):
@@ -105,7 +108,9 @@
     pieces = 4
     deep = width // pieces
     copy.wait()
-    mhalf[0] = local_ref[mine, :] + mrecv0[...]
+    copy_count.wait()
+    mhalf[0, 0:32] = local_ref[mine, :] + mrecv0[...]
+    mhalf[0, 32:40] = count[...] + crecv[...]
     for a in range(3):
         waits = [copies.start(mhalf.at[a], mrecv.at[a, o - 1], device(moved(at, a, o), core)) for o in (1, 2, 3)]
         first += jnp.dot(
@@ -114,9 +119,10 @@
         for w in waits:
             w.wait()
         mhalf[a + 1] = mhalf[a] + mrecv[a, 0] + mrecv[a, 1] + mrecv[a, 2]
-    mhalf[4] = mhalf[3] * (1.0 / 128.0)
-    mean_ref[mine, :] = mhalf[4]
-    copy = copies.start(mhalf.at[4], mean_ref.at[mine], partner)
+    count_ref[...] = mhalf[3, 32:40]
+    mhalf[4, 0:32] = mhalf[3, 0:32] * (1.0 / 128.0)
+    mean_ref[mine, :] = mhalf[4, 0:32]
+    copy = copies.start(mhalf.at[4, pl.ds(0, 32)], mean_ref.at[mine], partner)
     first += jnp.dot(c_ref[:, 3 * deep :], b_ref[3 * deep :, :], preferred_element_type=F32)
     first_t = first.T.astype(BF16)
     copy.wait()
@@ -244,13 +250,15 @@
     copies.start(view, view, partner).wait()
 
 
-def gram_and_square(samples, basis_start, n_total):
+def gram_and_square(samples, basis_start, labels, n_total):
     scratch = [
         pltpu.VMEM((256, 8192), BF16),
         pltpu.VMEM((64, 128), F32),
-        pltpu.VMEM((5, 32, 128), F32),
+        pltpu.VMEM((8, 128), F32),
+        pltpu.VMEM((8, 128), F32),
+        pltpu.VMEM((5, 40, 128), F32),
         pltpu.VMEM((32, 128), F32),
-        pltpu.VMEM((3, 3, 32, 128), F32),
+        pltpu.VMEM((3, 3, 40, 128), F32),
         pltpu.VMEM((16, 8192), BF16),
         pltpu.VMEM((4, 4, 4, 256, 128), BF16),
         pltpu.VMEM((4, 4, 4, 128, 128), BF16),
@@ -267,8 +275,8 @@
         pltpu.VMEM((2, 32, 128), F32),
         pltpu.VMEM((4, 2, 8, 128), F32),
         pltpu.VMEM((2, 8, 128), F32),
-        pltpu.SemaphoreType.DMA((56,)),
-        pltpu.SemaphoreType.DMA((56,)),
+        pltpu.SemaphoreType.DMA((57,)),
+        pltpu.SemaphoreType.DMA((57,)),
     ]
     return pl.pallas_call(
         functools.partial(gram_kernel, n_total),
@@ -276,13 +284,14 @@
             jax.ShapeDtypeStruct((256, 128), F32),
             jax.ShapeDtypeStruct((2, 256, 128), F32),
             jax.ShapeDtypeStruct((64, 128), F32),
+            jax.ShapeDtypeStruct((8, 128), F32),
         ),
-        in_specs=[VMEM, VMEM],
-        out_specs=(VMEM, VMEM, VMEM),
+        in_specs=[VMEM, VMEM, VMEM],
+        out_specs=(VMEM, VMEM, VMEM, VMEM),
         scratch_shapes=scratch,
         compiler_params=pltpu.CompilerParams(collective_id=0, has_side_effects=True, vmem_limit_bytes=LIMIT),
         name="gram",
-    )(samples, basis_start)
+    )(samples, basis_start, labels.reshape(1, 256))
 
 
 def small_inverse(t):
@@ -388,122 +397,151 @@
     return out.reshape(8192, 256)
 
 
+STEPS = ((0, 0, 0), (3, 0, 0), (0, 0, 3), (0, 1, 0), (2, 0, 0), (0, 3, 3), (3, 0, 1), (1, 1, 0), (0, 2, 3), (0, 0, 2), (2, 0, 1), (0, 2, 0))
+PARENTS = ((0, 0, 0), (0, 0, 0), (0, 0, 0), (3, 0, 0), (0, 0, 3), (3, 0, 0), (0, 1, 0), (0, 3, 3), (0, 0, 3), (2, 0, 0), (0, 1, 0))
+
+
+def difference(a, b):
+    return tuple((i - j) % 4 for i, j in zip(a, b))
+
+
+def panel_plan():
+    parent = [None, *[STEPS.index(p) for p in PARENTS]]
+    depth = [0] * len(STEPS)
+    for s in range(1, len(STEPS)):
+        depth[s] = depth[parent[s]] + 1
+    best = {}
+    for r, row in enumerate(STEPS):
+        for c, column in enumerate(STEPS):
+            d = difference(row, column)
+            cost = (max(depth[r], depth[c]), depth[r] + depth[c], r)
+            if d not in best or cost < best[d][0]:
+                best[d] = (cost, r, c)
+    units = sorted((cost[0], r, c) for cost, r, c in best.values())
+    assert len(units) == 64
+    return parent, depth, units
+
+
 def proof_kernel(
-    n_total, width_ref, p_ref, label_ref, out_ref,
-    rowp, colp, negrow, acc_all, acc_ref, pay, got, send, recv,
+    n_total, width_ref, n_ref_ref, p_ref, label_ref, out_ref,
+    blocks, columns, rows_ref, acc, got, send, recv,
 ):
     at, core = place()
-    x, y, z = at
-    z_lo, z_hi = z % 2, z // 2
+    other = 1 - core
     copies = Copies(send, recv)
-    partner = device(at, 1 - core)
-    me_row, me_col = lax.axis_index("row"), lax.axis_index("col")
-    rows = [((x + o) % 4, (z_hi + h) % 2) for h in (0, 1) for o in (0, 1, 2, 3)]
-    cols = [((y + o) % 4, (z_lo + h) % 2) for h in (0, 1) for o in (0, 1, 2, 3)]
-    row_devices = [device((rx, y, rh * 2 + z_lo), core) for rx, rh in rows]
-    col_devices = [device((x, cy, z_hi * 2 + cl), core) for cy, cl in cols]
-    greet([partner, *row_devices[1:], *col_devices[1:]])
-
+    partner = device(at, other)
+    parent, depth, units = panel_plan()
+    neighbours = [device(moved(at, a, o), core) for a in range(3) for o in (1, 3)]
+    greet([partner, *neighbours])
+
+    def toward(step):
+        return device(tuple((c + i) % 4 for c, i in zip(at, step)), core)
+
+    p = p_ref[...]
+    wide = p.astype(F32)
+    norm = jnp.broadcast_to(jnp.sum(wide * wide, 1, keepdims=True) * -0.5, (256, 128)).T
+    norm = jnp.concatenate([norm[:128, :128], norm[:128, 128:]], 1)[0:1]
+    high = norm.astype(BF16).astype(F32)
+    middle = (norm - high).astype(BF16).astype(F32)
+    low = (norm - high) - middle
     is_ref = (label_ref[...] == 0).astype(F32)
-    mine_row, mine_col = rowp.at[me_col], colp.at[me_row]
-    tail = jnp.broadcast_to(is_ref, (16, 256)).astype(BF16)
-    mine_row[0:256, :] = p_ref[...]
-    mine_row[256:272, :] = tail
-    mine_col[0:256, :] = p_ref[...]
-    mine_col[256:272, :] = tail
-    row_waits = [copies.start(mine_row, mine_row, d) for d in row_devices[1:]]
-    col_waits = [copies.start(mine_col, mine_col, d) for d in col_devices[1:]]
-    core_waits = [copies.start(mine_col, mine_col, partner)]
-    for (cy, cl), o, h, w in zip(cols[1:], (1, 2, 3, 0, 1, 2, 3), (0, 0, 0, 1, 1, 1, 1), col_waits):
-        w.wait()
-        slot = ((y + 4 - o) % 4) * 4 + ((z_lo + h) % 2) * 2 + core
-        view = colp.at[slot]
-        core_waits.append(copies.start(view, view, partner))
-    for w in row_waits:
-        w.wait()
+    ids = lax.broadcasted_iota(jnp.int32, (16, 256), 0)
+    tail = jnp.where(ids == 0, is_ref, jnp.where(ids == 1, high, jnp.where(ids == 2, middle, jnp.where(ids == 3, low, 0.0))))
+    blocks[0, core, 0:256, :] = p
+    blocks[0, core, 256:272, :] = tail.astype(BF16)
+
+    edges, cores = {}, {}
+
+    def hand_on(s):
+        view = blocks.at[s, core]
+        for child in range(1, len(STEPS)):
+            if parent[child] == s:
+                target = toward(difference(STEPS[s], STEPS[child]))
+                edges[child] = copies.start(view, blocks.at[child, core], target)
+        cores[s] = copies.start(view, view, partner)
 
     scale = 1.4426950408889634 / (128.0 * jnp.exp2(jnp.full((1, 256), width_ref[0], jnp.int32).astype(F32)))
-    ones = jnp.ones((8, 256), F32)
-    for q in range(8):
-        p = rowp[q, 0:256, :].astype(F32)
-        norm = lax.dot_general(ones, p * p, (((1,), (1,)), ((), ())), precision=HIGHEST, preferred_element_type=F32)
-        negrow[q] = norm * -0.5
-        acc_all[q] = jnp.zeros((8, 256), F32)
-        acc_ref[q] = jnp.zeros((8, 256), F32)
-    for w in core_waits:
-        w.wait()
-
-    def column(r, count):
-        block = colp[r, 0:256, :]
-        p = block.astype(F32)
-        half_norm = jnp.sum(p * p, 1, keepdims=True) * -0.5
-        mark_row = colp[r, 256:272, :].astype(F32)[0:1]
-        mark = jnp.concatenate(
-            [jnp.broadcast_to(mark_row[:, :128], (128, 128)).T, jnp.broadcast_to(mark_row[:, 128:], (128, 128)).T], 0
-        )
-        mark = jnp.concatenate([mark, mark], 1)
-
-        def row_block(q, carry):
-            inner = lax.dot_general(
-                block, rowp[q, 0:256, :], (((1,), (1,)), ((), ())), preferred_element_type=F32
-            )
-            value = jnp.exp2(((inner + half_norm) + negrow[q][0:1]) * scale)
-            acc_all[q] += jnp.sum(value.reshape(32, 8, 256), 0)
-            acc_ref[q] += jnp.sum((value * mark).reshape(32, 8, 256), 0)
-            return carry
-
-        lax.fori_loop(0, 8, row_block, 0)
-        return count + mark_row
-
-    count = lax.fori_loop(0, 16, column, jnp.zeros((1, 256), F32))
-    ids = lax.broadcasted_iota(jnp.int32, (8, 256), 0)
-    for q in range(8):
-        total = jnp.sum(acc_all[q], 0, keepdims=True)
-        refs = jnp.sum(acc_ref[q], 0, keepdims=True)
-        pay[q] = jnp.where(ids == 0, total, jnp.where(ids == 1, refs, count))
-    waits = []
-    for (rx, rh), d in zip(rows[1:], row_devices[1:]):
-        waits.append(copies.start(pay.at[rh * 4 + rx], got.at[me_col], d))
-    got[me_col] = pay[me_col]
-    for w in waits:
-        w.wait()
-    total = jnp.sum(got[...], 0)
-    row_sums, ref_sums = total[0:1], total[1:2]
-    n_ref = jnp.sum(total[2:3], 1, keepdims=True)
+    ids = lax.broadcasted_iota(jnp.int32, (16, 256), 0)
+    lanes = lax.broadcasted_iota(jnp.int32, (16, 256), 1)
+    select = jnp.where(lanes < 128, jnp.where((ids > 0) & (ids < 4), 1.0, 0.0), jnp.where(ids == 0, 1.0, 0.0)).astype(BF16)
+
+    def prepare(s):
+        for k in range(2):
+            ends = blocks[s, k, 256:272, :].astype(F32).T.astype(BF16)
+            columns[s, k] = jnp.dot(ends, select, preferred_element_type=F32)
+        ends = blocks[s, core, 256:272, :].astype(F32)
+        rows_ref[s] = jnp.broadcast_to((ends[1:2] + ends[2:3]) + ends[3:4], (8, 256))
+
+    for s in range(len(STEPS)):
+        acc[s, 0] = jnp.zeros((8, 256), F32)
+        acc[s, 1] = jnp.zeros((8, 256), F32)
+    hand_on(0)
+    for level in range(max(depth) + 1):
+        here = [s for s in range(len(STEPS)) if depth[s] == level]
+        for s in here:
+            if s:
+                edges[s].wait()
+                hand_on(s)
+        for s in here:
+            cores[s].wait()
+            prepare(s)
+        for _, r, c in [u for u in units if u[0] == level]:
+            row_norm = rows_ref[r][0:1]
+            rows = blocks[r, core, 0:256, :]
+            total, refs = acc[r, 0], acc[r, 1]
+            for k in range(2):
+                inner = lax.dot_general(
+                    blocks[c, k, 0:256, :], rows, (((1,), (1,)), ((), ())), preferred_element_type=F32
+                )
+                norm, mark = columns[c, k, :, :128], columns[c, k, :, 128:]
+                norm, mark = jnp.concatenate([norm, norm], 1), jnp.concatenate([mark, mark], 1)
+                value = jnp.exp2(((inner + norm) + row_norm) * scale)
+                total += jnp.sum(value.reshape(32, 8, 256), 0)
+                refs += jnp.sum((value * mark).reshape(32, 8, 256), 0)
+            acc[r, 0], acc[r, 1] = total, refs
+
+    for level in range(max(depth), 0, -1):
+        here = [s for s in range(1, len(STEPS)) if depth[s] == level]
+        waits = [copies.start(acc.at[s], got.at[s], toward(difference(STEPS[s], STEPS[parent[s]]))) for s in here]
+        for s, w in zip(here, waits):
+            w.wait()
+            acc[parent[s]] += got[s]
+    row_sums = jnp.sum(acc[0, 0], 0, keepdims=True)
+    ref_sums = jnp.sum(acc[0, 1], 0, keepdims=True)
+    n_ref = n_ref_ref[0:1, 0:1]
     n_cur = n_total - n_ref
     proof = (ref_sums / n_ref - (row_sums - ref_sums) / n_cur) / (row_sums / n_total)
     out_ref[...] = jnp.broadcast_to(proof, (8, 256))
 
 
-def proof_values(projected, labels, width_index, n_total):
+def proof_values(projected, labels, width_index, n_ref, n_total):
+    count = len(STEPS)
     out = pl.pallas_call(
         functools.partial(proof_kernel, n_total),
         out_shape=jax.ShapeDtypeStruct((8, 256), F32),
-        in_specs=[pl.BlockSpec(memory_space=pltpu.SMEM), VMEM, VMEM],
+        in_specs=[pl.BlockSpec(memory_space=pltpu.SMEM), VMEM, VMEM, VMEM],
         out_specs=VMEM,
         scratch_shapes=[
-            pltpu.VMEM((8, 272, 256), BF16),
-            pltpu.VMEM((16, 272, 256), BF16),
-            pltpu.VMEM((8, 8, 256), F32),
-            pltpu.VMEM((8, 8, 256), F32),
-            pltpu.VMEM((8, 8, 256), F32),
-            pltpu.VMEM((8, 8, 256), F32),
-            pltpu.VMEM((8, 8, 256), F32),
-            pltpu.SemaphoreType.DMA((29,)),
-            pltpu.SemaphoreType.DMA((29,)),
+            pltpu.VMEM((count, 2, 272, 256), BF16),
+            pltpu.VMEM((count, 2, 256, 256), F32),
+            pltpu.VMEM((count, 8, 256), F32),
+            pltpu.VMEM((count, 2, 8, 256), F32),
+            pltpu.VMEM((count, 2, 8, 256), F32),
+            pltpu.SemaphoreType.DMA((3 * count - 2,)),
+            pltpu.SemaphoreType.DMA((3 * count - 2,)),
         ],
         compiler_params=pltpu.CompilerParams(collective_id=2, has_side_effects=True, vmem_limit_bytes=LIMIT),
         name="proof",
-    )(width_index.reshape(1), projected, labels.reshape(1, 256))
+    )(width_index.reshape(1), n_ref, projected, labels.reshape(1, 256))
     return out[0]
 
 
 def local(n_total, samples, labels, basis_start, width_index):
-    g, square, mean = gram_and_square(samples, basis_start, n_total)
+    g, square, mean, n_ref = gram_and_square(samples, basis_start, labels, n_total)
     basis = gather_basis(g, square)
     centred = (samples - mean.reshape(1, 8192)).astype(BF16)
     projected = jnp.dot(centred, basis, preferred_element_type=F32).astype(BF16)
-    proof = proof_values(projected, labels, width_index, n_total)
+    proof = proof_values(projected, labels, width_index, n_ref, n_total)
     return projected, proof, basis
 
 

time: 217 us -> 178 us (0.82)
  Pallas kernels: 205 us -> 165 us
    pallas_call x1, Pallas kernels: 76.7 us -> 36.7 us  [proof_values(): pl.pallas_call(functools.partial(proof_kernel, n_total), out_shape=jax.Sh...]
where the time goes in v3:
time: 178 us; the launch traced here: 177 us
  Pallas kernels  165 us (93%)
  local copies, waits for them, and re-layouts  5.73 us (3%)
  matrix products  5.38 us (3%)
    pallas_call x1, Pallas kernels, gram_and_square(): pl.pallas_call(functools.partial(gram_kernel, n_total), out_shape=(jax.Sh...  83.8 us
    pallas_call x1, Pallas kernels, gather_basis(): pl.pallas_call(basis_kernel, out_shape=jax.ShapeDtypeStruct((4, 4, 4, 2,...  44.5 us
    pallas_call x1, Pallas kernels, proof_values(): pl.pallas_call(functools.partial(proof_kernel, n_total), out_shape=jax.Sh...  36.7 us
    dot_general x1, matrix products, local(): projected = jnp.dot(centred, basis, preferred_element_type=F32).astype(BF16)  5.38 us
    unnamed x3, local copies, waits for them, and re-layouts  4.47 us

profile of v3, /device:TPU:0, one launch (start us, length us, event | category | flops | bytes accessed | tf_op | source)
XLA Modules:
  0.0 177.5 jit_solution(11073416653910102656)
XLA Ops:
  0.6 83.8 %gram.1 = (f32[256,128]{1,0:T(8,128)}, f32[2,256,128]{2,1,0:T(8,128)}, f32[64,128]{1,0:T(8,128)}, f32[8,128]{1,0:T(8,128)}) custom-call(bf16[256,8192]{1,0:T(8,128)(2,1)} %x_ref.1, bf16[8192,256]{1,0:T(8,128)(2,1)} %b_ref.1, s32[1,256]{1,0:T(1,128)} %bitcast.9), custom_call_target="tpu_custom_call" | custom-call | tf_op jit(solution)/shard_map/gram/pallas_call | solution.py:281
  84.5 0.0 copy-start
  84.5 44.5 %basis.1 = bf16[4,4,4,2,64,256]{5,4,3,2,1,0:T(8,128)(2,1)} custom-call(f32[256,128]{1,0:T(8,128)} %get-tuple-element.8.g_ref, f32[2,256,128]{2,1,0:T(8,128)} %get-tuple-element.9.s_ref), custom_call_target="tpu_custom_call" | custom-call | tf_op jit(solution)/shard_map/basis/pallas_call | solution.py:388
  129.0 0.0 copy-done
  129.0 5.4 %fusion.2.p_ref = bf16[256,256]{1,0:T(8,128)(2,1)} fusion(bf16[8192,256]{1,0:T(8,128)(2,1)} %bitcast.7, bf16[256,8192]{1,0:T(8,128)(2,1)} %x_ref.1, f32[8192]{0:T(1024)S(1)} %bitcast.12), kind=kOutput, calls=%fused_computation.3 | convolution fusion | flops 1080098816 | bytes 8552448 | tf_op jit(solution)/shard_map/dot_general | solution.py:543
  135.0 36.7 %proof.1 = f32[8,256]{1,0:T(8,128)} custom-call(s32[1]{0:T(128)} %bitcast.6.width_ref, f32[8,128]{1,0:T(8,128)} %get-tuple-element.10.n_ref_ref, bf16[256,256]{1,0:T(8,128)(2,1)} %fusion.2.p_ref, s32[1,256]{1,0:T(1,128)} %bitcast.10), custom_call_target="tpu_custom_call" | custom-call | tf_op jit(solution)/shard_map/proof/pallas_call | solution.py:519
  171.8 1.3 slice.3
  173.0 4.5 %copy.9 = bf16[8192,256]{1,0:T(8,128)(2,1)} copy(bf16[8192,256]{1,0:T(8,128)(2,1)} %bitcast.8) | data formatting | bytes 8388608
Async XLA Ops:
  84.5 44.5 %copy-start = (f32[64,128]{1,0:T(8,128)S(1)}, f32[64,128]{1,0:T(8,128)}, u32[]{:S(2)}) copy-start(f32[64,128]{1,0:T(8,128)} %get-tuple-element.7) | copy-start | bytes 98308

commit v4 on v3

--- a/solution.py
+++ b/solution.py
@@ -1,4 +1,5 @@
 import functools
+import itertools
 
 import jax
 import jax.numpy as jnp
@@ -15,7 +16,6 @@
 LIMIT = 60 * 1024 * 1024
 
 PARTS = ((0, 48, (0, 1, 2)), (48, 48, (1, 2, 0)), (96, 32, (2, 0, 1)))
-GATHER = ((0, 32, (2, 1, 0)), (32, 16, (0, 2, 1)), (48, 16, (1, 0, 2)))
 
 
 def place():
@@ -356,47 +356,6 @@
     lax.fori_loop(0, 8, panel, 0)
 
 
-def basis_kernel(g_ref, s_ref, out_ref, m_ref, send, recv):
-    at, core = place()
-    copies = Copies(send, recv)
-    partner = device(at, 1 - core)
-    greet([partner, *axis_peers(at, core)])
-    inverse_factor(s_ref, m_ref)
-    block = lax.dot_general(
-        g_ref[...], m_ref[:, 256:512], (((0,), (1,)), ((), ())), precision=HIGHEST, preferred_element_type=F32
-    ).astype(BF16)
-    out_ref[at[0], at[1], at[2], core] = jnp.where(core == 0, block[:64], block[64:])
-    for step in range(3):
-        waits = []
-        for start, size, order in GATHER:
-            fixed = order[step:]
-            view = out_ref.at[(*pick(fixed, at), core, slice(start, start + size))]
-            for o in (1, 2, 3):
-                waits.append(copies.start(view, view, device(moved(at, order[step], o), core)))
-        for w in waits:
-            w.wait()
-    waits = []
-    for o in range(4):
-        bx = (at[0] + o) % 4
-        view = out_ref.at[bx, :, :, core]
-        waits.append(copies.start(view, view, partner))
-    for w in waits:
-        w.wait()
-
-
-def gather_basis(g, square):
-    out = pl.pallas_call(
-        basis_kernel,
-        out_shape=jax.ShapeDtypeStruct((4, 4, 4, 2, 64, 256), BF16),
-        in_specs=[VMEM, VMEM],
-        out_specs=VMEM,
-        scratch_shapes=[pltpu.VMEM((256, 512), F32), pltpu.SemaphoreType.DMA((31,)), pltpu.SemaphoreType.DMA((31,))],
-        compiler_params=pltpu.CompilerParams(collective_id=1, has_side_effects=True, vmem_limit_bytes=LIMIT),
-        name="basis",
-    )(g, square)
-    return out.reshape(8192, 256)
-
-
 STEPS = ((0, 0, 0), (3, 0, 0), (0, 0, 3), (0, 1, 0), (2, 0, 0), (0, 3, 3), (3, 0, 1), (1, 1, 0), (0, 2, 3), (0, 0, 2), (2, 0, 1), (0, 2, 0))
 PARENTS = ((0, 0, 0), (0, 0, 0), (0, 0, 0), (3, 0, 0), (0, 0, 3), (3, 0, 0), (0, 1, 0), (0, 3, 3), (0, 0, 3), (2, 0, 0), (0, 1, 0))
 
@@ -422,9 +381,28 @@
     return parent, depth, units
 
 
-def proof_kernel(
-    n_total, width_ref, n_ref_ref, p_ref, label_ref, out_ref,
-    blocks, columns, rows_ref, acc, got, send, recv,
+def spanning_tree():
+    def far(step):
+        return sum(min(c, 4 - c) for c in step)
+
+    steps = sorted(itertools.product(range(4), repeat=3), key=lambda step: (far(step), step))
+    load = {(a, o): 0 for a in range(3) for o in (1, 3)}
+    parent = [None]
+    for step in steps[1:]:
+        choices = []
+        for (a, o), used in load.items():
+            before = moved(step, a, 4 - o)
+            if far(before) == far(step) - 1:
+                choices.append((used, a, o, steps.index(before)))
+        _, a, o, before = min(choices)
+        load[a, o] += 1
+        parent.append(before)
+    return steps, parent, [far(step) for step in steps]
+
+
+def project_kernel(
+    n_total, width_ref, g_ref, s_ref, x_ref, mean_ref, n_ref_ref, label_ref, basis_ref, proj_ref, out_ref,
+    m_ref, p_acc, blocks, columns, rows_ref, acc, got, send, recv,
 ):
     at, core = place()
     other = 1 - core
@@ -434,10 +412,57 @@
     neighbours = [device(moved(at, a, o), core) for a in range(3) for o in (1, 3)]
     greet([partner, *neighbours])
 
+    def moved_by(step):
+        return tuple((c + i) % 4 for c, i in zip(at, step))
+
     def toward(step):
-        return device(tuple((c + i) % 4 for c, i in zip(at, step)), core)
-
-    p = p_ref[...]
+        return device(moved_by(step), core)
+
+    inverse_factor(s_ref, m_ref)
+    block = lax.dot_general(
+        g_ref[...], m_ref[:, 256:512], (((0,), (1,)), ((), ())), precision=HIGHEST, preferred_element_type=F32
+    ).astype(BF16)
+    basis_ref[(at[0] * 4 + at[1]) * 4 + at[2]] = block
+
+    steps, source, level_of = spanning_tree()
+    half = pl.ds(pl.multiple_of(core * 64, 64), 64)
+
+    def chip(s):
+        x, y, z = moved_by(steps[s])
+        return (x * 4 + y) * 4 + z
+
+    links, across = {}, {}
+    p_acc[...] = jnp.zeros_like(p_acc)
+
+    def add_level(level):
+        total = p_acc[...]
+        for s in range(64):
+            if level_of[s] == level:
+                if s:
+                    across[s].wait()
+                b = chip(s)
+                lanes = pl.ds(pl.multiple_of(b * 128, 128), 128)
+                centred = (x_ref[:, lanes].astype(F32) - mean_ref[pl.ds(b, 1), :]).astype(BF16)
+                total += jnp.dot(centred, basis_ref[b], preferred_element_type=F32)
+        p_acc[...] = total
+
+    for level in range(7):
+        for s in range(64):
+            if level_of[s] != level:
+                continue
+            if s:
+                links[s].wait()
+            view = basis_ref.at[chip(s), half, :]
+            for child in range(1, 64):
+                if source[child] == s:
+                    links[child] = copies.start(view, view, toward(difference(steps[s], steps[child])))
+            if s:
+                across[s] = copies.start(view, view, partner)
+        if level:
+            add_level(level - 1)
+    add_level(6)
+    p = p_acc[...].astype(BF16)
+    proj_ref[...] = p
     wide = p.astype(F32)
     norm = jnp.broadcast_to(jnp.sum(wide * wide, 1, keepdims=True) * -0.5, (256, 128)).T
     norm = jnp.concatenate([norm[:128, :128], norm[:128, 128:]], 1)[0:1]
@@ -514,34 +539,38 @@
     out_ref[...] = jnp.broadcast_to(proof, (8, 256))
 
 
-def proof_values(projected, labels, width_index, n_ref, n_total):
+def project_and_prove(g, square, samples, mean, n_ref, labels, width_index, n_total):
     count = len(STEPS)
-    out = pl.pallas_call(
-        functools.partial(proof_kernel, n_total),
-        out_shape=jax.ShapeDtypeStruct((8, 256), F32),
-        in_specs=[pl.BlockSpec(memory_space=pltpu.SMEM), VMEM, VMEM, VMEM],
-        out_specs=VMEM,
+    copies = 126 + 3 * count - 2
+    basis, projected, proof = pl.pallas_call(
+        functools.partial(project_kernel, n_total),
+        out_shape=(
+            jax.ShapeDtypeStruct((64, 128, 256), BF16),
+            jax.ShapeDtypeStruct((256, 256), BF16),
+            jax.ShapeDtypeStruct((8, 256), F32),
+        ),
+        in_specs=[pl.BlockSpec(memory_space=pltpu.SMEM), *[VMEM] * 6],
+        out_specs=(VMEM, VMEM, VMEM),
         scratch_shapes=[
+            pltpu.VMEM((256, 512), F32),
+            pltpu.VMEM((256, 256), F32),
             pltpu.VMEM((count, 2, 272, 256), BF16),
             pltpu.VMEM((count, 2, 256, 256), F32),
             pltpu.VMEM((count, 8, 256), F32),
             pltpu.VMEM((count, 2, 8, 256), F32),
             pltpu.VMEM((count, 2, 8, 256), F32),
-            pltpu.SemaphoreType.DMA((3 * count - 2,)),
-            pltpu.SemaphoreType.DMA((3 * count - 2,)),
+            pltpu.SemaphoreType.DMA((copies,)),
+            pltpu.SemaphoreType.DMA((copies,)),
         ],
-        compiler_params=pltpu.CompilerParams(collective_id=2, has_side_effects=True, vmem_limit_bytes=LIMIT),
-        name="proof",
-    )(width_index.reshape(1), n_ref, projected, labels.reshape(1, 256))
-    return out[0]
+        compiler_params=pltpu.CompilerParams(collective_id=1, has_side_effects=True, vmem_limit_bytes=LIMIT),
+        name="project",
+    )(width_index.reshape(1), g, square, samples, mean, n_ref, labels.reshape(1, 256))
+    return basis.reshape(8192, 256), projected, proof[0]
 
 
 def local(n_total, samples, labels, basis_start, width_index):
     g, square, mean, n_ref = gram_and_square(samples, basis_start, labels, n_total)
-    basis = gather_basis(g, square)
-    centred = (samples - mean.reshape(1, 8192)).astype(BF16)
-    projected = jnp.dot(centred, basis, preferred_element_type=F32).astype(BF16)
-    proof = proof_values(projected, labels, width_index, n_ref, n_total)
+    basis, projected, proof = project_and_prove(g, square, samples, mean, n_ref, labels, width_index, n_total)
     return projected, proof, basis
 
 

time: 178 us -> 172 us (0.966)
  matrix products: 5.38 us -> 0 us
  Pallas kernels: 165 us -> 163 us
    dot_general x1 -> x0, matrix products: 5.38 us -> none  [local(): projected = jnp.dot(centred, basis, preferred_element_type=F32).astype(BF16)]
    pallas_call x2 -> x1, Pallas kernels: 81.2 us -> 79.2 us  [project_and_prove(): pl.pallas_call(functools.partial(project_kernel, n_total), out_shape=(jax...]
    unnamed x3 -> x2, local copies, waits for them, and re-layouts: 4.47 us -> 6.04 us
where the time goes in v4:
time: 172 us
  Pallas kernels  163 us (95%)
  local copies, waits for them, and re-layouts  7.3 us (4%)
    pallas_call x1, Pallas kernels, gram_and_square(): pl.pallas_call(functools.partial(gram_kernel, n_total), out_shape=(jax.Sh...  83.8 us
    pallas_call x1, Pallas kernels, project_and_prove(): pl.pallas_call(functools.partial(project_kernel, n_total), out_shape=(jax...  79.2 us
    unnamed x2, local copies, waits for them, and re-layouts  6.04 us

profile of v4, /device:TPU:0, one launch (start us, length us, event | category | flops | bytes accessed | tf_op | source)
XLA Modules:
  0.0 171.6 jit_solution(17539565970420392890)
XLA Ops:
  1.3 83.8 %gram.1 = (f32[256,128]{1,0:T(8,128)}, f32[2,256,128]{2,1,0:T(8,128)}, f32[64,128]{1,0:T(8,128)}, f32[8,128]{1,0:T(8,128)}) custom-call(bf16[256,8192]{1,0:T(8,128)(2,1)} %x_ref.3, bf16[8192,256]{1,0:T(8,128)(2,1)} %b_ref.1, s32[1,256]{1,0:T(1,128)} %bitcast.6), custom_call_target="tpu_custom_call" | custom-call | tf_op jit(solution)/shard_map/gram/pallas_call | solution.py:281
  85.1 79.2 %project.1 = (bf16[64,128,256]{2,1,0:T(8,128)(2,1)}, bf16[256,256]{1,0:T(8,128)(2,1)}, f32[8,256]{1,0:T(8,128)}) custom-call(s32[1]{0:T(128)} %bitcast.4.width_ref, f32[256,128]{1,0:T(8,128)} %get-tuple-element.10.g_ref, f32[2,256,128]{2,1,0:T(8,128)} %get-tuple-element.11.s_ref, bf16[256,8192]{1,0:T(8,128)(2,1)} %x_ref.3, ...), custom_call_target="tpu_custom_call" | custom-call | tf_op jit(solution)/shard_map/project/pallas_call | solution.py:545
  164.3 1.3 slice.3
  165.6 1.6 copy.10
  167.2 4.5 %copy.11 = bf16[8192,256]{1,0:T(8,128)(2,1)} copy(bf16[8192,256]{1,0:T(8,128)(2,1)} %bitcast.5) | data formatting | bytes 8388608

commit v5 on v4

--- a/solution.py
+++ b/solution.py
@@ -71,8 +71,8 @@
 
 def gram_kernel(
     n_total, x_ref, b_ref, label_ref, g_ref, s_ref, mean_ref, count_ref,
-    c_ref, local_ref, count, crecv, mhalf, mrecv0, mrecv, daug, gt, half, recv0,
-    r1a, r1b, r1c, t1a, t1b, t1c, r2a, r2b, r2c, t2a, t2b, t2c, r3a, r3b, r3c,
+    c_ref, local_ref, theirs_ref, note, note_recv, mhalf, mrecv, delta_ref, daug, gt, half, recv0,
+    q1a, q1b, q1c, o1a, o1b, o1c, t1a, t1b, t1c, q2a, q2b, q2c, o2a, o2b, o2c, t2a, t2b, t2c, r3a, r3b, r3c,
     gme, s_half, sr0, sr1, ss1, sr2, ss2, send, recv,
 ):
     at, core = place()
@@ -82,128 +82,155 @@
     partner = device(at, other)
     greet([partner, *axis_peers(at, core)])
     n_local, width = x_ref.shape
-
-    @pl.loop(0, width // 256)
+    step = 512
+
+    @pl.loop(0, width // step)
     def _(j):
-        lanes = pl.ds(pl.multiple_of(j * 256, 256), 256)
+        lanes = pl.ds(pl.multiple_of(j * step, step), step)
         m = jnp.sum(x_ref[:, lanes].astype(F32), 0, keepdims=True) * (1.0 / n_local)
-        local_ref[pl.ds(2 * j, 1), :] = m[:, :128]
-        local_ref[pl.ds(2 * j + 1, 1), :] = m[:, 128:]
+        for i in range(step // 128):
+            local_ref[pl.ds(step // 128 * j + i, 1), :] = m[:, i * 128 : (i + 1) * 128]
+
+    copy = copies.start(local_ref, theirs_ref, partner)
+    ids = lax.broadcasted_iota(jnp.int32, (16, step), 0)
+
+    @pl.loop(0, width // step)
+    def _(j):
+        lanes = pl.ds(pl.multiple_of(j * step, step), step)
+        m = jnp.concatenate([local_ref[pl.ds(step // 128 * j + i, 1), :] for i in range(step // 128)], 1)
+        c_ref[0:n_local, lanes] = (x_ref[:, lanes].astype(F32) - m).astype(BF16)
+        high = m.astype(BF16).astype(F32)
+        middle = (m - high).astype(BF16).astype(F32)
+        low = (m - high) - middle
+        tile = jnp.where(ids == 0, high, jnp.where(ids == 1, middle, jnp.where(ids == 2, low, 0.0)))
+        c_ref[n_local : n_local + 16, lanes] = tile.astype(BF16)
+
+    first = jnp.dot(c_ref[...], b_ref[...], preferred_element_type=F32)
+    t_local = (first[n_local : n_local + 1] + first[n_local + 1 : n_local + 2]) + first[n_local + 2 : n_local + 3]
+    is_ref = (label_ref[...] == 0).astype(F32)
+    ids = lax.broadcasted_iota(jnp.int32, (8, 128), 0)
+    count = jnp.sum(is_ref, 1, keepdims=True)
+    note[...] = jnp.where(ids == 0, count, jnp.where(ids == 1, t_local[:, :128], jnp.where(ids == 2, t_local[:, 128:], 0.0)))
+    copy_note = copies.start(note, note_recv, partner)
+    first_t = first[:n_local].T.astype(BF16)
+    far = pl.ds(pl.multiple_of(other * 128, 128), 128)
+    near = pl.ds(pl.multiple_of(core * 128, 128), 128)
+    halves = []
+
+    def gram_blocks(bx):
+        @pl.loop(0, 4)
+        def _(by):
+            lanes = pl.ds(pl.multiple_of((bx * 4 + by) * 512, 512), 512)
+            block = jnp.dot(first_t, c_ref[0:n_local, lanes], preferred_element_type=F32).astype(BF16)
+            for bz in range(4):
+                gt[bx, by, bz] = block[:, bz * 128 : (bz + 1) * 128]
+
+        halves.append(copies.start(gt.at[bx, :, :, far, :], recv0.at[bx], partner))
 
     mine = pl.ds(pl.multiple_of(core * 32, 32), 32)
-    theirs = pl.ds(pl.multiple_of(other * 32, 32), 32)
-    copy = copies.start(local_ref.at[theirs], mrecv0, partner)
-    is_ref = (label_ref[...] == 0).astype(F32)
-    count[...] = jnp.broadcast_to(jnp.sum(is_ref, 1, keepdims=True), (8, 128))
-    copy_count = copies.start(count, crecv, partner)
-
-    @pl.loop(0, width // 256)
-    def _(j):
-        lanes = pl.ds(pl.multiple_of(j * 256, 256), 256)
-        rows = local_ref[pl.ds(2 * j, 2), :]
-        m = jnp.concatenate([rows[0:1], rows[1:2]], 1)
-        c_ref[:, lanes] = (x_ref[:, lanes].astype(F32) - m).astype(BF16)
-
-    first = jnp.zeros((n_local, b_ref.shape[1]), F32)
-    pieces = 4
-    deep = width // pieces
     copy.wait()
-    copy_count.wait()
-    mhalf[0, 0:32] = local_ref[mine, :] + mrecv0[...]
-    mhalf[0, 32:40] = count[...] + crecv[...]
+    copy_note.wait()
+    mhalf[0, 0:32] = local_ref[mine, :] + theirs_ref[mine, :]
+    mhalf[0, 32:40] = note[...] + note_recv[...]
     for a in range(3):
         waits = [copies.start(mhalf.at[a], mrecv.at[a, o - 1], device(moved(at, a, o), core)) for o in (1, 2, 3)]
-        first += jnp.dot(
-            c_ref[:, a * deep : (a + 1) * deep], b_ref[a * deep : (a + 1) * deep, :], preferred_element_type=F32
-        )
+        gram_blocks(a)
+        if a == 2:
+            gram_blocks(3)
         for w in waits:
             w.wait()
         mhalf[a + 1] = mhalf[a] + mrecv[a, 0] + mrecv[a, 1] + mrecv[a, 2]
-    count_ref[...] = mhalf[3, 32:40]
+    totals = mhalf[3, 32:40]
+    count_ref[...] = totals
     mhalf[4, 0:32] = mhalf[3, 0:32] * (1.0 / 128.0)
     mean_ref[mine, :] = mhalf[4, 0:32]
     copy = copies.start(mhalf.at[4, pl.ds(0, 32)], mean_ref.at[mine], partner)
-    first += jnp.dot(c_ref[:, 3 * deep :], b_ref[3 * deep :, :], preferred_element_type=F32)
-    first_t = first.T.astype(BF16)
+
+    mean_t = totals * (1.0 / 128.0)
+    ids = lax.broadcasted_iota(jnp.int32, (16, 256), 0)
+    taug = jnp.zeros((16, 256), F32)
+    for k, tile in enumerate((note[...], note_recv[...])):
+        tau = (tile - mean_t) * float(n_local)
+        tau = jnp.concatenate([tau[1:2], tau[2:3]], 1)
+        high = tau.astype(BF16).astype(F32)
+        taug = jnp.where((ids == 3 * k) | (ids == 3 * k + 1), high, jnp.where(ids == 3 * k + 2, tau - high, taug))
+    taug_t = taug.T
+    taug_t = jnp.where(core == 0, taug_t[:128], taug_t[128:]).astype(BF16)
     copy.wait()
-
-    ids = lax.broadcasted_iota(jnp.int32, (16, 128), 0)
-
-    @pl.loop(0, width // 128)
-    def _(j):
-        delta = local_ref[pl.ds(j, 1), :] - mean_ref[pl.ds(j, 1), :]
+    delta_ref[...] = jnp.zeros_like(delta_ref)
+    for k, source in enumerate((local_ref, theirs_ref)):
+        delta = source[...] - mean_ref[...]
         high = delta.astype(BF16).astype(F32)
-        low = delta - high
-        tile = jnp.where(ids == 1, low, jnp.where((ids == 0) | (ids == 2), high, 0.0))
-        daug[:, pl.ds(pl.multiple_of(j * 128, 128), 128)] = tile.astype(BF16)
-
-    tau = jnp.dot(daug[...], b_ref[...], preferred_element_type=F32)
-    tau = (tau[0:1] + tau[1:2]) * float(n_local)
-    t_high = tau.astype(BF16).astype(F32)
-    ids = lax.broadcasted_iota(jnp.int32, (16, 256), 0)
-    taug = jnp.where(ids == 2, tau - t_high, jnp.where(ids < 2, t_high, 0.0))
-    taug_t = taug.T.astype(BF16)
-
-    @pl.loop(0, width // 256)
-    def _(j):
-        lanes = pl.ds(pl.multiple_of(j * 256, 256), 256)
-        block = jnp.dot(first_t, c_ref[:, lanes], preferred_element_type=F32)
-        block += jnp.dot(taug_t, daug[:, lanes], preferred_element_type=F32)
-        block = block.astype(BF16)
-        bx, by, bz = j // 8, (j // 2) % 4, (j % 2) * 2
-        gt[bx, by, bz] = block[:, :128]
-        gt[bx, by, bz + 1] = block[:, 128:]
-
-    near = pl.ds(pl.multiple_of(core * 128, 128), 128)
-    far = pl.ds(pl.multiple_of(other * 128, 128), 128)
-    copies.start(gt.at[:, :, :, far, :], recv0, partner).wait()
-
-    @pl.loop(0, 64)
-    def _(j):
-        bx, by, bz = j // 16, (j // 4) % 4, j % 4
-        half[bx, by, bz] = (gt[bx, by, bz, near, :].astype(F32) + recv0[bx, by, bz].astype(F32)).astype(BF16)
-
-    parts = list(zip(PARTS, (r1a, r1b, r1c), (t1a, t1b, t1c), (r2a, r2b, r2c), (t2a, t2b, t2c), (r3a, r3b, r3c)))
+        delta_ref[:, 3 * k, :] = high
+        delta_ref[:, 3 * k + 1, :] = delta - high
+        delta_ref[:, 3 * k + 2, :] = high
+    daug[...] = delta_ref[...].astype(BF16)
+
+    for bx in range(4):
+        halves[bx].wait()
+
+        @pl.loop(0, 4)
+        def _(by):
+            for bz in range(4):
+                extra = jnp.dot(taug_t, daug[(bx * 4 + by) * 4 + bz], preferred_element_type=F32)
+                both = gt[bx, by, bz, near, :].astype(F32) + recv0[bx, by, bz].astype(F32)
+                half[bx, by, bz] = (both + extra).astype(BF16)
+
+    def exchange(parts, dtype, source, incoming, outgoing, result):
+        todo = []
+        for i, (axis, size) in enumerate(parts):
+            up, down = device(moved(at, axis, 1), core), device(moved(at, axis, 3), core)
+            chunks = [source(i, (at[axis] + o) % 4) for o in range(4)]
+            low, high = pl.ds(0, 2), pl.ds(2, 2)
+            box = incoming[i]
+            first_up = copies.start(chunks[2].at[low], box.at[0], up)
+            first_down = copies.start(chunks[2].at[high], box.at[1], down)
+            near_up = copies.start(chunks[1].at[high], box.at[2], up)
+            near_down = copies.start(chunks[3].at[low], box.at[3], down)
+            todo.append((up, down, chunks, first_up, first_down, near_up, near_down))
+        last = []
+        for i, (up, down, chunks, first_up, first_down, _, _) in enumerate(todo):
+            box, out = incoming[i], outgoing[i]
+            first_up.wait()
+            out[0] = chunks[1][0:2] + box[0]
+            add_up = copies.start(out.at[0], box.at[4], up)
+            first_down.wait()
+            out[1] = chunks[3][2:4] + box[1]
+            add_down = copies.start(out.at[1], box.at[5], down)
+            last.append((add_up, add_down))
+        for i, (_, _, chunks, _, _, near_up, near_down) in enumerate(todo):
+            box = incoming[i]
+            near_up.wait()
+            near_down.wait()
+            for w in last[i]:
+                w.wait()
+            own = chunks[0]
+            result[i][0:2] = (own[0:2].astype(F32) + box[3].astype(F32)) + box[4].astype(F32)
+            result[i][2:4] = (own[2:4].astype(F32) + box[2].astype(F32)) + box[5].astype(F32)
+
+    orders = [order for _, _, order in PARTS]
+    t1s, t2s = (t1a, t1b, t1c), (t2a, t2b, t2c)
+
+    def stage_one(i, k):
+        start, size, order = PARTS[i]
+        to = tuple(k for _ in range(3))
+        return half.at[pick(order[:1], to, slice(start, start + size))]
+
+    def stage_two(i, k):
+        _, _, order = PARTS[i]
+        left = [a for a in range(3) if a != order[0]]
+        return t1s[i].at[k] if left[0] == order[1] else t1s[i].at[:, k]
+
+    exchange([(o[0], 0) for o in orders], BF16, stage_one, (q1a, q1b, q1c), (o1a, o1b, o1c), t1s)
+    exchange([(o[1], 0) for o in orders], F32, stage_two, (q2a, q2b, q2c), (o2a, o2b, o2c), t2s)
     waits = []
-    for (start, size, order), r1, _, _, _, _ in parts:
-        rows = slice(start, start + size)
-        for o in (1, 2, 3):
-            to = moved(at, order[0], o)
-            waits.append(copies.start(half.at[pick(order[:1], to, rows)], r1.at[o - 1], device(to, core)))
-    for w in waits:
-        w.wait()
-    waits = []
-    for (start, size, order), r1, t1, r2, _, _ in parts:
-        rows = slice(start, start + size)
-        own = half.at[pick(order[:1], at, rows)]
-
-        @pl.loop(0, 16)
-        def _(j):
-            u, v = j // 4, j % 4
-            t1[u, v] = (own[u, v].astype(F32) + r1[0, u, v].astype(F32)) + (
-                r1[1, u, v].astype(F32) + r1[2, u, v].astype(F32)
-            )
-
-        left = [a for a in range(3) if a != order[0]]
-        for o in (1, 2, 3):
-            to = moved(at, order[1], o)
-            index = (to[order[1]],) if left[0] == order[1] else (slice(None), to[order[1]])
-            waits.append(copies.start(t1.at[index], r2.at[o - 1], device(to, core)))
-    for w in waits:
-        w.wait()
-    waits = []
-    for (start, size, order), _, t1, r2, t2, r3 in parts:
-        left = [a for a in range(3) if a != order[0]]
-        first_left = left[0] == order[1]
-        for k in range(4):
-            own = t1[at[order[1]], k] if first_left else t1[k, at[order[1]]]
-            t2[k] = (own + r2[0, k]) + (r2[1, k] + r2[2, k])
+    for (start, size, order), t2, r3 in zip(PARTS, t2s, (r3a, r3b, r3c)):
         for o in (1, 2, 3):
             to = moved(at, order[2], o)
             waits.append(copies.start(t2.at[to[order[2]]], r3.at[o - 1], device(to, core)))
     for w in waits:
         w.wait()
-    for (start, size, order), _, _, _, t2, r3 in parts:
+    for (start, size, order), t2, r3 in zip(PARTS, t2s, (r3a, r3b, r3c)):
         total = (t2[at[order[2]]] + r3[0]) + (r3[1] + r3[2])
         gme[start : start + size, :] = total * (1.0 / n_total)
     g_ref[near, :] = gme[...]
@@ -252,20 +279,23 @@
 
 def gram_and_square(samples, basis_start, labels, n_total):
     scratch = [
-        pltpu.VMEM((256, 8192), BF16),
+        pltpu.VMEM((272, 8192), BF16),
+        pltpu.VMEM((64, 128), F32),
         pltpu.VMEM((64, 128), F32),
         pltpu.VMEM((8, 128), F32),
         pltpu.VMEM((8, 128), F32),
         pltpu.VMEM((5, 40, 128), F32),
-        pltpu.VMEM((32, 128), F32),
         pltpu.VMEM((3, 3, 40, 128), F32),
-        pltpu.VMEM((16, 8192), BF16),
+        pltpu.VMEM((64, 16, 128), F32),
+        pltpu.VMEM((64, 16, 128), BF16),
         pltpu.VMEM((4, 4, 4, 256, 128), BF16),
         pltpu.VMEM((4, 4, 4, 128, 128), BF16),
         pltpu.VMEM((4, 4, 4, 128, 128), BF16),
-        *[pltpu.VMEM((3, 4, 4, size, 128), BF16) for _, size, _ in PARTS],
+        *[pltpu.VMEM((6, 2, 4, size, 128), BF16) for _, size, _ in PARTS],
+        *[pltpu.VMEM((2, 2, 4, size, 128), BF16) for _, size, _ in PARTS],
         *[pltpu.VMEM((4, 4, size, 128), F32) for _, size, _ in PARTS],
-        *[pltpu.VMEM((3, 4, size, 128), F32) for _, size, _ in PARTS],
+        *[pltpu.VMEM((6, 2, size, 128), F32) for _, size, _ in PARTS],
+        *[pltpu.VMEM((2, 2, size, 128), F32) for _, size, _ in PARTS],
         *[pltpu.VMEM((4, size, 128), F32) for _, size, _ in PARTS],
         *[pltpu.VMEM((3, size, 128), F32) for _, size, _ in PARTS],
         pltpu.VMEM((128, 128), F32),
@@ -275,8 +305,8 @@
         pltpu.VMEM((2, 32, 128), F32),
         pltpu.VMEM((4, 2, 8, 128), F32),
         pltpu.VMEM((2, 8, 128), F32),
-        pltpu.SemaphoreType.DMA((57,)),
-        pltpu.SemaphoreType.DMA((57,)),
+        pltpu.SemaphoreType.DMA((78,)),
+        pltpu.SemaphoreType.DMA((78,)),
     ]
     return pl.pallas_call(
         functools.partial(gram_kernel, n_total),

time: 172 us -> 162 us (0.942)
  Pallas kernels: 163 us -> 153 us
    pallas_call x1, Pallas kernels: 83.8 us -> 73.7 us  [gram_and_square(): pl.pallas_call(functools.partial(gram_kernel, n_total), out_shape=(jax.Sh...]
where the time goes in v5:
time: 162 us; the launch traced here: 161 us
  Pallas kernels  153 us (94%)
  local copies, waits for them, and re-layouts  7.3 us (5%)
    pallas_call x1, Pallas kernels, project_and_prove(): pl.pallas_call(functools.partial(project_kernel, n_total), out_shape=(jax...  79 us
    pallas_call x1, Pallas kernels, gram_and_square(): pl.pallas_call(functools.partial(gram_kernel, n_total), out_shape=(jax.Sh...  73.7 us
    unnamed x2, local copies, waits for them, and re-layouts  6.04 us

profile of v5, /device:TPU:0, one launch (start us, length us, event | category | flops | bytes accessed | tf_op | source)
XLA Modules:
  0.0 161.3 jit_solution(8206848763436189703)
XLA Ops:
  1.3 73.7 %gram.1 = (f32[256,128]{1,0:T(8,128)}, f32[2,256,128]{2,1,0:T(8,128)}, f32[64,128]{1,0:T(8,128)}, f32[8,128]{1,0:T(8,128)}) custom-call(bf16[256,8192]{1,0:T(8,128)(2,1)} %x_ref.3, bf16[8192,256]{1,0:T(8,128)(2,1)} %b_ref.1, s32[1,256]{1,0:T(1,128)} %bitcast.6), custom_call_target="tpu_custom_call" | custom-call | tf_op jit(solution)/shard_map/gram/pallas_call | solution.py:311
  75.0 79.0 %project.1 = (bf16[64,128,256]{2,1,0:T(8,128)(2,1)}, bf16[256,256]{1,0:T(8,128)(2,1)}, f32[8,256]{1,0:T(8,128)}) custom-call(s32[1]{0:T(128)} %bitcast.4.width_ref, f32[256,128]{1,0:T(8,128)} %get-tuple-element.10.g_ref, f32[2,256,128]{2,1,0:T(8,128)} %get-tuple-element.11.s_ref, bf16[256,8192]{1,0:T(8,128)(2,1)} %x_ref.3, ...), custom_call_target="tpu_custom_call" | custom-call | tf_op jit(solution)/shard_map/project/pallas_call | solution.py:575
  154.0 1.3 slice.3
  155.3 1.6 copy.10
  156.8 4.5 %copy.11 = bf16[8192,256]{1,0:T(8,128)(2,1)} copy(bf16[8192,256]{1,0:T(8,128)(2,1)} %bitcast.5) | data formatting | bytes 8388608

commit v6 on v5

--- a/solution.py
+++ b/solution.py
@@ -69,27 +69,27 @@
     return index if rows is None else (*index, rows)
 
 
-def gram_kernel(
-    n_total, x_ref, b_ref, label_ref, g_ref, s_ref, mean_ref, count_ref,
-    c_ref, local_ref, theirs_ref, note, note_recv, mhalf, mrecv, delta_ref, daug, gt, half, recv0,
+def gram_part(
+    n_total, at, core, copies, x_loads, b_load, x_ref, b_ref, label_ref, g_ref, s_ref, mean_ref, count_ref,
+    c_ref, local_ref, theirs_ref, note, note_recv, mhalf, mrecv, notes, nrecv, delta_ref, daug, gt, half, recv0,
     q1a, q1b, q1c, o1a, o1b, o1c, t1a, t1b, t1c, q2a, q2b, q2c, o2a, o2b, o2c, t2a, t2b, t2c, r3a, r3b, r3c,
-    gme, s_half, sr0, sr1, ss1, sr2, ss2, send, recv,
+    gme, s_half, sr0, sr1, ss1, sr2, ss2,
 ):
-    at, core = place()
-    x, y, z = at
     other = 1 - core
-    copies = Copies(send, recv)
     partner = device(at, other)
-    greet([partner, *axis_peers(at, core)])
     n_local, width = x_ref.shape
     step = 512
-
-    @pl.loop(0, width // step)
-    def _(j):
-        lanes = pl.ds(pl.multiple_of(j * step, step), step)
-        m = jnp.sum(x_ref[:, lanes].astype(F32), 0, keepdims=True) * (1.0 / n_local)
-        for i in range(step // 128):
-            local_ref[pl.ds(step // 128 * j + i, 1), :] = m[:, i * 128 : (i + 1) * 128]
+    turns = width // step // len(x_loads)
+
+    for chunk, load in enumerate(x_loads):
+        load.wait()
+
+        @pl.loop(chunk * turns, (chunk + 1) * turns)
+        def _(j):
+            lanes = pl.ds(pl.multiple_of(j * step, step), step)
+            m = jnp.sum(x_ref[:, lanes].astype(F32), 0, keepdims=True) * (1.0 / n_local)
+            for i in range(step // 128):
+                local_ref[pl.ds(step // 128 * j + i, 1), :] = m[:, i * 128 : (i + 1) * 128]
 
     copy = copies.start(local_ref, theirs_ref, partner)
     ids = lax.broadcasted_iota(jnp.int32, (16, step), 0)
@@ -104,6 +104,20 @@
         low = (m - high) - middle
         tile = jnp.where(ids == 0, high, jnp.where(ids == 1, middle, jnp.where(ids == 2, low, 0.0)))
         c_ref[n_local : n_local + 16, lanes] = tile.astype(BF16)
+
+    def start_axis(values, landing, a):
+        return [copies.start(values.at[a], landing.at[a, o - 1], device(moved(at, a, o), core)) for o in (1, 2, 3)]
+
+    def end_axis(values, landing, a, waits):
+        for w in waits:
+            w.wait()
+        values[a + 1] = values[a] + landing[a, 0] + landing[a, 1] + landing[a, 2]
+
+    mine = pl.ds(pl.multiple_of(core * 32, 32), 32)
+    copy.wait()
+    mhalf[0] = local_ref[mine, :] + theirs_ref[mine, :]
+    mean_waits = start_axis(mhalf, mrecv, 0)
+    b_load.wait()
 
     first = jnp.dot(c_ref[...], b_ref[...], preferred_element_type=F32)
     t_local = (first[n_local : n_local + 1] + first[n_local + 1 : n_local + 2]) + first[n_local + 2 : n_local + 3]
@@ -127,24 +141,28 @@
 
         halves.append(copies.start(gt.at[bx, :, :, far, :], recv0.at[bx], partner))
 
-    mine = pl.ds(pl.multiple_of(core * 32, 32), 32)
-    copy.wait()
+    end_axis(mhalf, mrecv, 0, mean_waits)
+    mean_waits = start_axis(mhalf, mrecv, 1)
     copy_note.wait()
-    mhalf[0, 0:32] = local_ref[mine, :] + theirs_ref[mine, :]
-    mhalf[0, 32:40] = note[...] + note_recv[...]
-    for a in range(3):
-        waits = [copies.start(mhalf.at[a], mrecv.at[a, o - 1], device(moved(at, a, o), core)) for o in (1, 2, 3)]
-        gram_blocks(a)
-        if a == 2:
-            gram_blocks(3)
-        for w in waits:
-            w.wait()
-        mhalf[a + 1] = mhalf[a] + mrecv[a, 0] + mrecv[a, 1] + mrecv[a, 2]
-    totals = mhalf[3, 32:40]
+    notes[0] = note[...] + note_recv[...]
+    note_waits = start_axis(notes, nrecv, 0)
+    gram_blocks(0)
+    end_axis(mhalf, mrecv, 1, mean_waits)
+    mean_waits = start_axis(mhalf, mrecv, 2)
+    end_axis(notes, nrecv, 0, note_waits)
+    note_waits = start_axis(notes, nrecv, 1)
+    gram_blocks(1)
+    end_axis(mhalf, mrecv, 2, mean_waits)
+    mhalf[4] = mhalf[3] * (1.0 / 128.0)
+    mean_ref[mine, :] = mhalf[4]
+    copy = copies.start(mhalf.at[4], mean_ref.at[mine], partner)
+    end_axis(notes, nrecv, 1, note_waits)
+    note_waits = start_axis(notes, nrecv, 2)
+    gram_blocks(2)
+    gram_blocks(3)
+    end_axis(notes, nrecv, 2, note_waits)
+    totals = notes[3]
     count_ref[...] = totals
-    mhalf[4, 0:32] = mhalf[3, 0:32] * (1.0 / 128.0)
-    mean_ref[mine, :] = mhalf[4, 0:32]
-    copy = copies.start(mhalf.at[4, pl.ds(0, 32)], mean_ref.at[mine], partner)
 
     mean_t = totals * (1.0 / 128.0)
     ids = lax.broadcasted_iota(jnp.int32, (16, 256), 0)
@@ -241,51 +259,65 @@
     )
     s_half[0] = square[:, :128]
     s_half[1] = square[:, 128:]
+    plans = ((0, (0, 1, 2)), (1, (1, 2, 0)))
+
+    def band(h, position, size):
+        return pl.ds(pl.multiple_of(position * size, size), size)
+
     waits = []
-    for o in (1, 2, 3):
-        to = moved(at, 0, o)
-        rows = pl.ds(pl.multiple_of(to[0] * 32, 32), 32)
-        waits.append(copies.start(s_half.at[:, rows, :], sr0.at[o - 1], device(to, core)))
+    for h, order in plans:
+        for o in (1, 2, 3):
+            to = moved(at, order[0], o)
+            waits.append(
+                copies.start(s_half.at[h, band(h, to[order[0]], 32), :], sr0.at[h, o - 1], device(to, core))
+            )
     for w in waits:
         w.wait()
-    ss1[...] = (s_half[:, pl.ds(pl.multiple_of(x * 32, 32), 32), :] + sr0[0]) + (sr0[1] + sr0[2])
     waits = []
-    for o in (1, 2, 3):
-        to = moved(at, 1, o)
-        rows = pl.ds(pl.multiple_of(to[1] * 8, 8), 8)
-        waits.append(copies.start(ss1.at[:, rows, :], sr1.at[o - 1], device(to, core)))
+    for h, order in plans:
+        ss1[h] = (s_half[h, band(h, at[order[0]], 32), :] + sr0[h, 0]) + (sr0[h, 1] + sr0[h, 2])
+        for o in (1, 2, 3):
+            to = moved(at, order[1], o)
+            waits.append(copies.start(ss1.at[h, band(h, to[order[1]], 8), :], sr1.at[h, o - 1], device(to, core)))
     for w in waits:
         w.wait()
-    ss2[...] = (ss1[:, pl.ds(pl.multiple_of(y * 8, 8), 8), :] + sr1[0]) + (sr1[1] + sr1[2])
     waits = []
-    for o in (1, 2, 3):
-        waits.append(copies.start(ss2, sr2.at[z], device(moved(at, 2, o), core)))
-    sr2[z] = ss2[...]
+    for h, order in plans:
+        ss2[h] = (ss1[h, band(h, at[order[1]], 8), :] + sr1[h, 0]) + (sr1[h, 1] + sr1[h, 2])
+        for o in (1, 2, 3):
+            waits.append(copies.start(ss2.at[h], sr2.at[h, at[order[2]]], device(moved(at, order[2], o), core)))
+        sr2[h, at[order[2]]] = ss2[h]
     for w in waits:
         w.wait()
-    base = pl.multiple_of(core * 128 + x * 32 + y * 8, 8)
-    s_ref[:, pl.ds(base, 8), :] = (sr2[0] + sr2[1]) + (sr2[2] + sr2[3])
-    for axis, rows in (
-        (1, pl.ds(base, 8)),
-        (0, pl.ds(pl.multiple_of(core * 128 + x * 32, 32), 32)),
-    ):
-        view = s_ref.at[:, rows, :]
-        waits = [copies.start(view, view, device(moved(at, axis, o), core)) for o in (1, 2, 3)]
+    bases = [core * 128 + at[order[0]] * 32 + at[order[1]] * 8 for _, order in plans]
+    for (h, order), base in zip(plans, bases):
+        s_ref[h, pl.ds(pl.multiple_of(base, 8), 8), :] = (sr2[h, 0] + sr2[h, 1]) + (sr2[h, 2] + sr2[h, 3])
+    for level in (1, 0):
+        waits = []
+        for (h, order), base in zip(plans, bases):
+            if level:
+                rows = pl.ds(pl.multiple_of(base, 8), 8)
+            else:
+                rows = pl.ds(pl.multiple_of(core * 128 + at[order[0]] * 32, 32), 32)
+            view = s_ref.at[h, rows, :]
+            waits += [copies.start(view, view, device(moved(at, order[level], o), core)) for o in (1, 2, 3)]
         for w in waits:
             w.wait()
     view = s_ref.at[:, near, :]
     copies.start(view, view, partner).wait()
 
 
-def gram_and_square(samples, basis_start, labels, n_total):
-    scratch = [
+def gram_scratch():
+    return [
         pltpu.VMEM((272, 8192), BF16),
         pltpu.VMEM((64, 128), F32),
         pltpu.VMEM((64, 128), F32),
         pltpu.VMEM((8, 128), F32),
         pltpu.VMEM((8, 128), F32),
-        pltpu.VMEM((5, 40, 128), F32),
-        pltpu.VMEM((3, 3, 40, 128), F32),
+        pltpu.VMEM((5, 32, 128), F32),
+        pltpu.VMEM((3, 3, 32, 128), F32),
+        pltpu.VMEM((4, 8, 128), F32),
+        pltpu.VMEM((3, 3, 8, 128), F32),
         pltpu.VMEM((64, 16, 128), F32),
         pltpu.VMEM((64, 16, 128), BF16),
         pltpu.VMEM((4, 4, 4, 256, 128), BF16),
@@ -300,28 +332,12 @@
         *[pltpu.VMEM((3, size, 128), F32) for _, size, _ in PARTS],
         pltpu.VMEM((128, 128), F32),
         pltpu.VMEM((2, 128, 128), F32),
-        pltpu.VMEM((3, 2, 32, 128), F32),
-        pltpu.VMEM((3, 2, 8, 128), F32),
+        pltpu.VMEM((2, 3, 32, 128), F32),
+        pltpu.VMEM((2, 3, 8, 128), F32),
         pltpu.VMEM((2, 32, 128), F32),
-        pltpu.VMEM((4, 2, 8, 128), F32),
+        pltpu.VMEM((2, 4, 8, 128), F32),
         pltpu.VMEM((2, 8, 128), F32),
-        pltpu.SemaphoreType.DMA((78,)),
-        pltpu.SemaphoreType.DMA((78,)),
     ]
-    return pl.pallas_call(
-        functools.partial(gram_kernel, n_total),
-        out_shape=(
-            jax.ShapeDtypeStruct((256, 128), F32),
-            jax.ShapeDtypeStruct((2, 256, 128), F32),
-            jax.ShapeDtypeStruct((64, 128), F32),
-            jax.ShapeDtypeStruct((8, 128), F32),
-        ),
-        in_specs=[VMEM, VMEM, VMEM],
-        out_specs=(VMEM, VMEM, VMEM, VMEM),
-        scratch_shapes=scratch,
-        compiler_params=pltpu.CompilerParams(collective_id=0, has_side_effects=True, vmem_limit_bytes=LIMIT),
-        name="gram",
-    )(samples, basis_start, labels.reshape(1, 256))
 
 
 def small_inverse(t):
@@ -368,22 +384,22 @@
     m_ref[:, 256:512] = (r == c).astype(F32)
     lane = lax.broadcasted_iota(jnp.int32, (32, 128), 1)
     unit = (lane == lax.broadcasted_iota(jnp.int32, (32, 128), 0) + 32).astype(F32)
-    wide = lax.broadcasted_iota(jnp.int32, (32, 256), 1)
-
-    def panel(b, carry):
-        rows = pl.ds(pl.multiple_of(b * 32, 32), 32)
-        tile = m_ref[rows, pl.ds(pl.multiple_of((b // 4) * 128, 128), 128)]
-        tile = pltpu.roll(tile, (4 - b % 4) % 4 * 32, 1)
+    for b in range(8):
+        left = 128 * (b // 4)
+        rows, window = slice(32 * b, 32 * b + 32), slice(left, left + 384)
+        tile = m_ref[rows, left : left + 128]
+        if b % 4:
+            tile = pltpu.roll(tile, 128 - 32 * (b % 4), 1)
         tile = jnp.where(lane < 32, tile, unit)
         t = small_inverse([tile[8 * i : 8 * i + 8] for i in range(4)])
         inv = jnp.concatenate(t, 0)[:, 32:64]
-        w = jnp.dot(inv, m_ref[rows, :], precision=HIGHEST, preferred_element_type=F32)
-        left = jnp.where(wide >= (b + 1) * 32, w[:, :256], 0.0)
-        m_ref[...] -= lax.dot_general(left, w, (((0,), (0,)), ((), ())), precision=HIGHEST, preferred_element_type=F32)
-        m_ref[rows, :] = w
-        return carry
-
-    lax.fori_loop(0, 8, panel, 0)
+        w = jnp.dot(inv, m_ref[rows, window], precision=HIGHEST, preferred_element_type=F32)
+        if b < 7:
+            update = lax.dot_general(
+                w[:, : 256 - left], w, (((0,), (0,)), ((), ())), precision=HIGHEST, preferred_element_type=F32
+            )
+            m_ref[32 * b + 32 :, window] -= update[32 * b + 32 - left :]
+        m_ref[rows, window] = w
 
 
 STEPS = ((0, 0, 0), (3, 0, 0), (0, 0, 3), (0, 1, 0), (2, 0, 0), (0, 3, 3), (3, 0, 1), (1, 1, 0), (0, 2, 3), (0, 0, 2), (2, 0, 1), (0, 2, 0))
@@ -430,17 +446,14 @@
     return steps, parent, [far(step) for step in steps]
 
 
-def project_kernel(
-    n_total, width_ref, g_ref, s_ref, x_ref, mean_ref, n_ref_ref, label_ref, basis_ref, proj_ref, out_ref,
-    m_ref, p_acc, blocks, columns, rows_ref, acc, got, send, recv,
+def project_part(
+    n_total, at, core, copies, width_ref, label_ref, x_ref, g_ref, s_ref, mean_ref, n_ref_ref,
+    basis_out, proj_ref, out_ref, basis_sem,
+    basis_ref, m_ref, p_acc, blocks, columns, rows_ref, acc, got,
 ):
-    at, core = place()
     other = 1 - core
-    copies = Copies(send, recv)
     partner = device(at, other)
     parent, depth, units = panel_plan()
-    neighbours = [device(moved(at, a, o), core) for a in range(3) for o in (1, 3)]
-    greet([partner, *neighbours])
 
     def moved_by(step):
         return tuple((c + i) % 4 for c, i in zip(at, step))
@@ -491,6 +504,8 @@
         if level:
             add_level(level - 1)
     add_level(6)
+    basis_copy = pltpu.make_async_copy(basis_ref, basis_out, basis_sem)
+    basis_copy.start()
     p = p_acc[...].astype(BF16)
     proj_ref[...] = p
     wide = p.astype(F32)
@@ -567,41 +582,112 @@
     n_cur = n_total - n_ref
     proof = (ref_sums / n_ref - (row_sums - ref_sums) / n_cur) / (row_sums / n_total)
     out_ref[...] = jnp.broadcast_to(proof, (8, 256))
-
-
-def project_and_prove(g, square, samples, mean, n_ref, labels, width_index, n_total):
+    basis_copy.wait()
+
+
+def project_scratch():
     count = len(STEPS)
-    copies = 126 + 3 * count - 2
+    return [
+        pltpu.VMEM((64, 128, 256), BF16),
+        pltpu.VMEM((256, 512), F32),
+        pltpu.VMEM((256, 256), F32),
+        pltpu.VMEM((count, 2, 272, 256), BF16),
+        pltpu.VMEM((count, 2, 256, 256), F32),
+        pltpu.VMEM((count, 8, 256), F32),
+        pltpu.VMEM((count, 2, 8, 256), F32),
+        pltpu.VMEM((count, 2, 8, 256), F32),
+    ]
+
+
+def drift_kernel(
+    n_total, n_gram, width_ref, x_hbm, b_hbm, label_ref, basis_out, proj_ref, out_ref,
+    x_ref, b_ref, g_ref, s_ref, mean_ref, count_ref, load_sem, send, recv, *scratch,
+):
+    chunks = 4
+    lanes = x_ref.shape[1] // chunks
+    loads = []
+    for i in range(chunks):
+        part = slice(i * lanes, (i + 1) * lanes)
+        loads.append(pltpu.make_async_copy(x_hbm.at[:, part], x_ref.at[:, part], load_sem.at[i]))
+    b_load = pltpu.make_async_copy(b_hbm, b_ref, load_sem.at[chunks])
+    for load in (*loads, b_load):
+        load.start()
+    at, core = place()
+    copies = Copies(send, recv)
+    greet([device(at, 1 - core), *axis_peers(at, core)])
+    gram_part(
+        n_total, at, core, copies, loads, b_load, x_ref, b_ref, label_ref, g_ref, s_ref, mean_ref, count_ref,
+        *scratch[:n_gram],
+    )
+    project_part(
+        n_total, at, core, copies, width_ref, label_ref, x_ref, g_ref, s_ref, mean_ref, count_ref,
+        basis_out, proj_ref, out_ref, load_sem.at[chunks + 1],
+        *scratch[n_gram:],
+    )
+
+
+def hand_out_kernel(basis, projected, proof, basis_out, projected_out, proof_out):
+    basis_out[...] = basis[...]
+
+    @pl.when(pl.program_id(0) == 0)
+    def _():
+        projected_out[...] = projected[...]
+        proof_out[...] = proof[0:1, :]
+
+
+def hand_out(basis, projected, proof):
+    tiles = 8
+    tile = pl.BlockSpec((basis.shape[0] // tiles, basis.shape[1]), lambda i: (i, 0))
+    whole = [pl.BlockSpec(a.shape, lambda i: (0, 0)) for a in (projected, proof)]
     basis, projected, proof = pl.pallas_call(
-        functools.partial(project_kernel, n_total),
+        hand_out_kernel,
+        grid=(tiles,),
+        out_shape=(
+            jax.ShapeDtypeStruct(basis.shape, basis.dtype),
+            jax.ShapeDtypeStruct(projected.shape, projected.dtype),
+            jax.ShapeDtypeStruct((1, 256), F32),
+        ),
+        in_specs=[tile, *whole],
+        out_specs=(tile, whole[0], pl.BlockSpec((1, 256), lambda i: (0, 0))),
+        name="hand_out",
+    )(basis, projected, proof)
+    return projected, proof.reshape(256), basis
+
+
+def local(n_total, samples, labels, basis_start, width_index):
+    gram, project = gram_scratch(), project_scratch()
+    n_copies = 102 + 126 + 3 * len(STEPS) - 2
+    basis, projected, proof = pl.pallas_call(
+        functools.partial(drift_kernel, n_total, len(gram)),
         out_shape=(
             jax.ShapeDtypeStruct((64, 128, 256), BF16),
             jax.ShapeDtypeStruct((256, 256), BF16),
             jax.ShapeDtypeStruct((8, 256), F32),
         ),
-        in_specs=[pl.BlockSpec(memory_space=pltpu.SMEM), *[VMEM] * 6],
-        out_specs=(VMEM, VMEM, VMEM),
+        in_specs=[
+            pl.BlockSpec(memory_space=pltpu.SMEM),
+            pl.BlockSpec(memory_space=pl.ANY),
+            pl.BlockSpec(memory_space=pl.ANY),
+            VMEM,
+        ],
+        out_specs=(pl.BlockSpec(memory_space=pl.ANY), VMEM, VMEM),
         scratch_shapes=[
-            pltpu.VMEM((256, 512), F32),
-            pltpu.VMEM((256, 256), F32),
-            pltpu.VMEM((count, 2, 272, 256), BF16),
-            pltpu.VMEM((count, 2, 256, 256), F32),
-            pltpu.VMEM((count, 8, 256), F32),
-            pltpu.VMEM((count, 2, 8, 256), F32),
-            pltpu.VMEM((count, 2, 8, 256), F32),
-            pltpu.SemaphoreType.DMA((copies,)),
-            pltpu.SemaphoreType.DMA((copies,)),
+            pltpu.VMEM((256, 8192), BF16),
+            pltpu.VMEM((8192, 256), BF16),
+            pltpu.VMEM((256, 128), F32),
+            pltpu.VMEM((2, 256, 128), F32),
+            pltpu.VMEM((64, 128), F32),
+            pltpu.VMEM((8, 128), F32),
+            pltpu.SemaphoreType.DMA((6,)),
+            pltpu.SemaphoreType.DMA((n_copies,)),
+            pltpu.SemaphoreType.DMA((n_copies,)),
+            *gram,
+            *project,
         ],
-        compiler_params=pltpu.CompilerParams(collective_id=1, has_side_effects=True, vmem_limit_bytes=LIMIT),
-        name="project",
-    )(width_index.reshape(1), g, square, samples, mean, n_ref, labels.reshape(1, 256))
-    return basis.reshape(8192, 256), projected, proof[0]
-
-
-def local(n_total, samples, labels, basis_start, width_index):
-    g, square, mean, n_ref = gram_and_square(samples, basis_start, labels, n_total)
-    basis, projected, proof = project_and_prove(g, square, samples, mean, n_ref, labels, width_index, n_total)
-    return projected, proof, basis
+        compiler_params=pltpu.CompilerParams(collective_id=0, has_side_effects=True, vmem_limit_bytes=LIMIT),
+        name="drift",
+    )(width_index.reshape(1), samples, basis_start, labels.reshape(1, 256))
+    return hand_out(basis.reshape(8192, 256), projected, proof)
 
 
 def solution(mesh):

time: 162 us -> 150 us (0.926)
  local copies, waits for them, and re-layouts: 7.3 us -> 0 us
  Pallas kernels: 153 us -> 148 us
    unnamed x2 -> x0, local copies, waits for them, and re-layouts: 6.04 us -> none
    pallas_call x2, Pallas kernels: 153 us -> 148 us  [the longest x1 141 us: local(): pl.pallas_call(functools.partial(drift_kernel, n_total, len(gram)), out_s...]
where the time goes in v6:
time: 150 us; the launch traced here: 149 us
  Pallas kernels  148 us (99%)
    pallas_call x1, Pallas kernels, local(): pl.pallas_call(functools.partial(drift_kernel, n_total, len(gram)), out_s...  141 us
    pallas_call x1, Pallas kernels, hand_out(): pl.pallas_call(hand_out_kernel, grid=(tiles,), out_shape=(jax.ShapeDtypeS...  6.7 us

profile of v6, /device:TPU:0, one launch (start us, length us, event | category | flops | bytes accessed | tf_op | source)
XLA Modules:
  0.0 149.3 jit_solution(15484143398717359007)
XLA Ops:
  1.3 141.4 %drift.1 = (bf16[64,128,256]{2,1,0:T(8,128)(2,1)}, bf16[256,256]{1,0:T(8,128)(2,1)}, f32[8,256]{1,0:T(8,128)}) custom-call(s32[1]{0:T(128)} %bitcast.4.width_ref, bf16[256,8192]{1,0:T(8,128)(2,1)} %x_hbm.1, bf16[8192,256]{1,0:T(8,128)(2,1)} %b_hbm.1, s32[1,256]{1,0:T(1,128)} %bitcast.6), custom_call_target="tpu_custom_call" | custom-call | tf_op jit(solution)/shard_map/drift/pallas_call | solution.py:660
  142.6 6.7 %hand_out.1 = (bf16[8192,256]{1,0:T(8,128)(2,1)}, bf16[256,256]{1,0:T(8,128)(2,1)}, f32[1,256]{1,0:T(1,128)}) custom-call(bf16[8192,256]{1,0:T(8,128)(2,1)} %bitcast.5, bf16[256,256]{1,0:T(8,128)(2,1)} %get-tuple-element.10.projected, f32[8,256]{1,0:T(8,128)} %get-tuple-element.11.proof), custom_call_target="tpu_custom_call" | custom-call | tf_op jit(solution)/shard_map/hand_out/pallas_call | solution.py:642

commit v7 on v6

--- a/solution.py
+++ b/solution.py
@@ -13,7 +13,7 @@
 BF16 = jnp.bfloat16
 VMEM = pl.BlockSpec(memory_space=pltpu.VMEM)
 HIGHEST = lax.Precision.HIGHEST
-LIMIT = 60 * 1024 * 1024
+LIMIT = 48 * 1024 * 1024
 
 PARTS = ((0, 48, (0, 1, 2)), (48, 48, (1, 2, 0)), (96, 32, (2, 0, 1)))
 
@@ -70,7 +70,7 @@
 
 
 def gram_part(
-    n_total, at, core, copies, x_loads, b_load, x_ref, b_ref, label_ref, g_ref, s_ref, mean_ref, count_ref,
+    n_total, at, core, copies, gathering, gram_all, x_loads, b_load, x_ref, b_ref, label_ref, g_ref, s_ref, mean_ref, count_ref,
     c_ref, local_ref, theirs_ref, note, note_recv, mhalf, mrecv, notes, nrecv, delta_ref, daug, gt, half, recv0,
     q1a, q1b, q1c, o1a, o1b, o1c, t1a, t1b, t1c, q2a, q2b, q2c, o2a, o2b, o2c, t2a, t2b, t2c, r3a, r3b, r3c,
     gme, s_half, sr0, sr1, ss1, sr2, ss2,
@@ -253,6 +253,8 @@
         gme[start : start + size, :] = total * (1.0 / n_total)
     g_ref[near, :] = gme[...]
     copies.start(gme, g_ref.at[near], partner).wait()
+    gram_all[chip_number(at)] = g_ref[...].T
+    next(gathering)
 
     square = lax.dot_general(
         gme[...], g_ref[...], (((1,), (1,)), ((), ())), precision=HIGHEST, preferred_element_type=F32
@@ -287,6 +289,7 @@
         for o in (1, 2, 3):
             waits.append(copies.start(ss2.at[h], sr2.at[h, at[order[2]]], device(moved(at, order[2], o), core)))
         sr2[h, at[order[2]]] = ss2[h]
+    next(gathering)
     for w in waits:
         w.wait()
     bases = [core * 128 + at[order[0]] * 32 + at[order[1]] * 8 for _, order in plans]
@@ -304,7 +307,9 @@
         for w in waits:
             w.wait()
     view = s_ref.at[:, near, :]
-    copies.start(view, view, partner).wait()
+    copy = copies.start(view, view, partner)
+    next(gathering)
+    copy.wait()
 
 
 def gram_scratch():
@@ -376,7 +381,7 @@
     return t
 
 
-def inverse_factor(s_ref, m_ref):
+def inverse_factor(s_ref, m_ref, gathering):
     r = lax.broadcasted_iota(jnp.int32, (256, 256), 0)
     c = lax.broadcasted_iota(jnp.int32, (256, 256), 1)
     m_ref[:, 0:128] = s_ref[0]
@@ -400,6 +405,8 @@
             )
             m_ref[32 * b + 32 :, window] -= update[32 * b + 32 - left :]
         m_ref[rows, window] = w
+        if b in (2, 5, 7):
+            next(gathering)
 
 
 STEPS = ((0, 0, 0), (3, 0, 0), (0, 0, 3), (0, 1, 0), (2, 0, 0), (0, 3, 3), (3, 0, 1), (1, 1, 0), (0, 2, 3), (0, 0, 2), (2, 0, 1), (0, 2, 0))
@@ -446,64 +453,75 @@
     return steps, parent, [far(step) for step in steps]
 
 
-def project_part(
-    n_total, at, core, copies, width_ref, label_ref, x_ref, g_ref, s_ref, mean_ref, n_ref_ref,
-    basis_out, proj_ref, out_ref, basis_sem,
-    basis_ref, m_ref, p_acc, blocks, columns, rows_ref, acc, got,
-):
-    other = 1 - core
-    partner = device(at, other)
-    parent, depth, units = panel_plan()
+def chip_number(at):
+    return (at[0] * 4 + at[1]) * 4 + at[2]
+
+
+def gather(at, core, copies, ref):
+    steps, source, level_of = spanning_tree()
+    partner = device(at, 1 - core)
+    half = pl.ds(pl.multiple_of(core * 64, 64), 64)
 
     def moved_by(step):
         return tuple((c + i) % 4 for c, i in zip(at, step))
 
-    def toward(step):
-        return device(moved_by(step), core)
-
-    inverse_factor(s_ref, m_ref)
-    block = lax.dot_general(
-        g_ref[...], m_ref[:, 256:512], (((0,), (1,)), ((), ())), precision=HIGHEST, preferred_element_type=F32
-    ).astype(BF16)
-    basis_ref[(at[0] * 4 + at[1]) * 4 + at[2]] = block
-
-    steps, source, level_of = spanning_tree()
-    half = pl.ds(pl.multiple_of(core * 64, 64), 64)
-
-    def chip(s):
-        x, y, z = moved_by(steps[s])
-        return (x * 4 + y) * 4 + z
-
     links, across = {}, {}
-    p_acc[...] = jnp.zeros_like(p_acc)
-
-    def add_level(level):
-        total = p_acc[...]
-        for s in range(64):
-            if level_of[s] == level:
-                if s:
-                    across[s].wait()
-                b = chip(s)
-                lanes = pl.ds(pl.multiple_of(b * 128, 128), 128)
-                centred = (x_ref[:, lanes].astype(F32) - mean_ref[pl.ds(b, 1), :]).astype(BF16)
-                total += jnp.dot(centred, basis_ref[b], preferred_element_type=F32)
-        p_acc[...] = total
-
     for level in range(7):
         for s in range(64):
             if level_of[s] != level:
                 continue
             if s:
                 links[s].wait()
-            view = basis_ref.at[chip(s), half, :]
+            view = ref.at[chip_number(moved_by(steps[s])), half, :]
             for child in range(1, 64):
                 if source[child] == s:
-                    links[child] = copies.start(view, view, toward(difference(steps[s], steps[child])))
+                    target = device(moved_by(difference(steps[s], steps[child])), core)
+                    links[child] = copies.start(view, view, target)
             if s:
                 across[s] = copies.start(view, view, partner)
-        if level:
-            add_level(level - 1)
-    add_level(6)
+        yield
+    for s in range(1, 64):
+        across[s].wait()
+    yield
+
+
+def project_part(
+    n_total, at, core, copies, gathering, gram_all, basis_ref, width_ref, label_ref, x_ref, s_ref, mean_ref, n_ref_ref,
+    basis_out, proj_ref, out_ref, basis_sem,
+    m_ref, inv_high, inv_low, p_acc, blocks, columns, rows_ref, acc, got,
+):
+    other = 1 - core
+    partner = device(at, other)
+    parent, depth, units = panel_plan()
+
+    def toward(step):
+        return device(tuple((c + i) % 4 for c, i in zip(at, step)), core)
+
+    inverse_factor(s_ref, m_ref, gathering)
+    for _ in gathering:
+        pass
+    inverse_t = m_ref[:, 256:512].T
+    high = inverse_t.astype(BF16)
+    inv_high[...] = high
+    inv_low[...] = (inverse_t - high.astype(F32)).astype(BF16)
+    p_acc[...] = jnp.zeros_like(p_acc)
+
+    @pl.loop(0, 16)
+    def _(j):
+        chips = pl.ds(4 * j, 4)
+        gram = gram_all[chips].reshape(512, 256)
+        high = gram.astype(BF16)
+        low = (gram - high.astype(F32)).astype(BF16)
+        block = jnp.dot(low, inv_high[...], preferred_element_type=F32)
+        block += jnp.dot(high, inv_low[...], preferred_element_type=F32)
+        block += jnp.dot(high, inv_high[...], preferred_element_type=F32)
+        block = block.astype(BF16)
+        lanes = pl.ds(pl.multiple_of(j * 512, 512), 512)
+        basis_ref[lanes, :] = block
+        mean = jnp.concatenate([mean_ref[pl.ds(4 * j + i, 1), :] for i in range(4)], 1)
+        centred = (x_ref[:, lanes].astype(F32) - mean).astype(BF16)
+        p_acc[...] += jnp.dot(centred, block, preferred_element_type=F32)
+
     basis_copy = pltpu.make_async_copy(basis_ref, basis_out, basis_sem)
     basis_copy.start()
     p = p_acc[...].astype(BF16)
@@ -588,8 +606,9 @@
 def project_scratch():
     count = len(STEPS)
     return [
-        pltpu.VMEM((64, 128, 256), BF16),
         pltpu.VMEM((256, 512), F32),
+        pltpu.VMEM((256, 256), BF16),
+        pltpu.VMEM((256, 256), BF16),
         pltpu.VMEM((256, 256), F32),
         pltpu.VMEM((count, 2, 272, 256), BF16),
         pltpu.VMEM((count, 2, 256, 256), F32),
@@ -601,7 +620,7 @@
 
 def drift_kernel(
     n_total, n_gram, width_ref, x_hbm, b_hbm, label_ref, basis_out, proj_ref, out_ref,
-    x_ref, b_ref, g_ref, s_ref, mean_ref, count_ref, load_sem, send, recv, *scratch,
+    x_ref, b_ref, g_ref, s_ref, mean_ref, count_ref, gram_all, load_sem, send, recv, *scratch,
 ):
     chunks = 4
     lanes = x_ref.shape[1] // chunks
@@ -615,43 +634,40 @@
     at, core = place()
     copies = Copies(send, recv)
     greet([device(at, 1 - core), *axis_peers(at, core)])
+    gathering = gather(at, core, copies, gram_all)
     gram_part(
-        n_total, at, core, copies, loads, b_load, x_ref, b_ref, label_ref, g_ref, s_ref, mean_ref, count_ref,
+        n_total, at, core, copies, gathering, gram_all, loads, b_load, x_ref, b_ref, label_ref, g_ref, s_ref, mean_ref, count_ref,
         *scratch[:n_gram],
     )
     project_part(
-        n_total, at, core, copies, width_ref, label_ref, x_ref, g_ref, s_ref, mean_ref, count_ref,
+        n_total, at, core, copies, gathering, gram_all, b_ref, width_ref, label_ref, x_ref, s_ref, mean_ref, count_ref,
         basis_out, proj_ref, out_ref, load_sem.at[chunks + 1],
         *scratch[n_gram:],
     )
 
 
-def hand_out_kernel(basis, projected, proof, basis_out, projected_out, proof_out):
-    basis_out[...] = basis[...]
-
-    @pl.when(pl.program_id(0) == 0)
-    def _():
-        projected_out[...] = projected[...]
-        proof_out[...] = proof[0:1, :]
+def hand_out_kernel(basis, projected, proof, basis_out, projected_out, proof_out, sems):
+    moves = ((basis, basis_out), (projected, projected_out), (proof, proof_out))
+    waits = [pltpu.make_async_copy(src, dst, sems.at[i]) for i, (src, dst) in enumerate(moves)]
+    for w in waits:
+        w.start()
+    for w in waits:
+        w.wait()
 
 
 def hand_out(basis, projected, proof):
-    tiles = 8
-    tile = pl.BlockSpec((basis.shape[0] // tiles, basis.shape[1]), lambda i: (i, 0))
-    whole = [pl.BlockSpec(a.shape, lambda i: (0, 0)) for a in (projected, proof)]
+    arrays = (basis, projected, proof)
+    anywhere = [pl.BlockSpec(memory_space=pl.ANY)] * 3
     basis, projected, proof = pl.pallas_call(
         hand_out_kernel,
-        grid=(tiles,),
-        out_shape=(
-            jax.ShapeDtypeStruct(basis.shape, basis.dtype),
-            jax.ShapeDtypeStruct(projected.shape, projected.dtype),
-            jax.ShapeDtypeStruct((1, 256), F32),
-        ),
-        in_specs=[tile, *whole],
-        out_specs=(tile, whole[0], pl.BlockSpec((1, 256), lambda i: (0, 0))),
+        out_shape=tuple(jax.ShapeDtypeStruct(a.shape, a.dtype) for a in arrays),
+        in_specs=anywhere,
+        out_specs=tuple(anywhere),
+        scratch_shapes=[pltpu.SemaphoreType.DMA((3,))],
+        compiler_params=pltpu.CompilerParams(vmem_limit_bytes=8 * 1024 * 1024),
         name="hand_out",
-    )(basis, projected, proof)
-    return projected, proof.reshape(256), basis
+    )(*arrays)
+    return projected, proof[0], basis
 
 
 def local(n_total, samples, labels, basis_start, width_index):
@@ -660,7 +676,7 @@
     basis, projected, proof = pl.pallas_call(
         functools.partial(drift_kernel, n_total, len(gram)),
         out_shape=(
-            jax.ShapeDtypeStruct((64, 128, 256), BF16),
+            jax.ShapeDtypeStruct((8192, 256), BF16),
             jax.ShapeDtypeStruct((256, 256), BF16),
             jax.ShapeDtypeStruct((8, 256), F32),
         ),
@@ -678,6 +694,7 @@
             pltpu.VMEM((2, 256, 128), F32),
             pltpu.VMEM((64, 128), F32),
             pltpu.VMEM((8, 128), F32),
+            pltpu.VMEM((64, 128, 256), F32),
             pltpu.SemaphoreType.DMA((6,)),
             pltpu.SemaphoreType.DMA((n_copies,)),
             pltpu.SemaphoreType.DMA((n_copies,)),
@@ -687,7 +704,7 @@
         compiler_params=pltpu.CompilerParams(collective_id=0, has_side_effects=True, vmem_limit_bytes=LIMIT),
         name="drift",
     )(width_index.reshape(1), samples, basis_start, labels.reshape(1, 256))
-    return hand_out(basis.reshape(8192, 256), projected, proof)
+    return hand_out(basis, projected, proof)
 
 
 def solution(mesh):

time: 150 us -> 140 us (0.933)
  Pallas kernels: 148 us -> 138 us
    pallas_call x1, Pallas kernels: 141 us -> 136 us  [local(): pl.pallas_call(functools.partial(drift_kernel, n_total, len(gram)), out_s...]
    pallas_call x1, Pallas kernels: 6.7 us -> 2.07 us  [hand_out(): pl.pallas_call(hand_out_kernel, out_shape=tuple((jax.ShapeDtypeStruct(a.s...]
where the time goes in v7:
time: 140 us
  Pallas kernels  138 us (99%)
    pallas_call x1, Pallas kernels, local(): pl.pallas_call(functools.partial(drift_kernel, n_total, len(gram)), out_s...  136 us

profile of v7, /device:TPU:0, one launch (start us, length us, event | category | flops | bytes accessed | tf_op | source)
XLA Modules:
  0.0 140.3 jit_solution(16955923187020538211)
XLA Ops:
  1.3 0.0 copy-start
  1.3 0.7 copy-done
  2.0 135.7 %drift.1 = (bf16[8192,256]{1,0:T(8,128)(2,1)S(1)}, bf16[256,256]{1,0:T(8,128)(2,1)S(1)}, f32[8,256]{1,0:T(8,128)S(1)}) custom-call(s32[1]{0:T(128)} %bitcast.3.width_ref, bf16[256,8192]{1,0:T(8,128)(2,1)} %x_hbm.1, bf16[8192,256]{1,0:T(8,128)(2,1)} %b_hbm.1, s32[1,256]{1,0:T(1,128)S(1)} %bitcast.4), custom_call_target="tpu_custom_call" | custom-call | tf_op jit(solution)/shard_map/drift/pallas_call | solution.py:676
  137.7 2.1 %hand_out.1 = (bf16[8192,256]{1,0:T(8,128)(2,1)}, bf16[256,256]{1,0:T(8,128)(2,1)}, f32[8,256]{1,0:T(8,128)S(1)}) custom-call(bf16[8192,256]{1,0:T(8,128)(2,1)S(1)} %get-tuple-element.9.basis, bf16[256,256]{1,0:T(8,128)(2,1)S(1)} %get-tuple-element.10.projected, f32[8,256]{1,0:T(8,128)S(1)} %get-tuple-element.11.proof), custom_call_target="tpu_custom_call" | custom-call | tf_op jit(solution)/shard_map/hand_out/pallas_call | solution.py:661
  139.7 0.6 slice.3
Async XLA Ops:
  1.3 0.7 copy-start

commit v8 on v7

--- a/solution.py
+++ b/solution.py
@@ -588,12 +588,24 @@
                 refs += jnp.sum((value * mark).reshape(32, 8, 256), 0)
             acc[r, 0], acc[r, 1] = total, refs
 
-    for level in range(max(depth), 0, -1):
-        here = [s for s in range(1, len(STEPS)) if depth[s] == level]
-        waits = [copies.start(acc.at[s], got.at[s], toward(difference(STEPS[s], STEPS[parent[s]]))) for s in here]
-        for s, w in zip(here, waits):
-            w.wait()
-            acc[parent[s]] += got[s]
+    def axes(step):
+        return sum(c != 0 for c in step)
+
+    waits = []
+    for s in range(1, len(STEPS)):
+        if axes(STEPS[s]) == 2:
+            onto = [q for q in range(1, len(STEPS)) if axes(STEPS[q]) == 1 and axes(difference(STEPS[s], STEPS[q])) == 1][0]
+            waits.append((s, onto, copies.start(acc.at[s], got.at[s], toward(difference(STEPS[s], STEPS[onto])))))
+    for _, _, w in waits:
+        w.wait()
+    for s, onto, _ in waits:
+        acc[onto] += got[s]
+    straight = [s for s in range(1, len(STEPS)) if axes(STEPS[s]) == 1]
+    waits = [copies.start(acc.at[s], got.at[s], toward(STEPS[s])) for s in straight]
+    for w in waits:
+        w.wait()
+    for s in straight:
+        acc[0] += got[s]
     row_sums = jnp.sum(acc[0, 0], 0, keepdims=True)
     ref_sums = jnp.sum(acc[0, 1], 0, keepdims=True)
     n_ref = n_ref_ref[0:1, 0:1]

time: 140 us -> 138 us (0.986)
  Pallas kernels: 138 us -> 135 us
    pallas_call x1, Pallas kernels: 136 us -> 133 us  [local(): pl.pallas_call(functools.partial(drift_kernel, n_total, len(gram)), out_s...]
where the time goes in v8:
time: 138 us
  Pallas kernels  135 us (98%)
    pallas_call x1, Pallas kernels, local(): pl.pallas_call(functools.partial(drift_kernel, n_total, len(gram)), out_s...  133 us

profile of v8, /device:TPU:0, one launch (start us, length us, event | category | flops | bytes accessed | tf_op | source)
XLA Modules:
  0.0 138.0 jit_solution(3271163756261872267)
XLA Ops:
  1.3 0.0 copy-start
  1.3 0.7 copy-done
  2.0 133.3 %drift.1 = (bf16[8192,256]{1,0:T(8,128)(2,1)S(1)}, bf16[256,256]{1,0:T(8,128)(2,1)S(1)}, f32[8,256]{1,0:T(8,128)S(1)}) custom-call(s32[1]{0:T(128)} %bitcast.3.width_ref, bf16[256,8192]{1,0:T(8,128)(2,1)} %x_hbm.1, bf16[8192,256]{1,0:T(8,128)(2,1)} %b_hbm.1, s32[1,256]{1,0:T(1,128)S(1)} %bitcast.4), custom_call_target="tpu_custom_call" | custom-call | tf_op jit(solution)/shard_map/drift/pallas_call | solution.py:688
  135.3 2.1 %hand_out.1 = (bf16[8192,256]{1,0:T(8,128)(2,1)}, bf16[256,256]{1,0:T(8,128)(2,1)}, f32[8,256]{1,0:T(8,128)S(1)}) custom-call(bf16[8192,256]{1,0:T(8,128)(2,1)S(1)} %get-tuple-element.9.basis, bf16[256,256]{1,0:T(8,128)(2,1)S(1)} %get-tuple-element.10.projected, f32[8,256]{1,0:T(8,128)S(1)} %get-tuple-element.11.proof), custom_call_target="tpu_custom_call" | custom-call | tf_op jit(solution)/shard_map/hand_out/pallas_call | solution.py:673
  137.4 0.6 slice.3
Async XLA Ops:
  1.3 0.7 copy-start
